TPU v7x, 256 devices: a whole 4x4x8 slice. The times are simulated.
256 devices in a mesh: seq: 32 (over z, x), feat: 8 (over y, core).
Axes of the slice: x: 4, y: 4, z: 8, core: 2. Of those that a mesh axis runs over, the one named last changes fastest.
Arguments:
- teacher_states: bfloat16 [4, 32768, 3584], P(None, 'seq', 'feat')
- student_states: bfloat16 [32768, 2304], P('seq'), may hold values from -6 to 6
- projection: bfloat16 [4, 2304, 3584], P(None, 'seq', 'feat'), may hold values from -0.125 to 0.125
- layer_pick: int32 [4], replicated, may hold values from 0 to 3, each once
- validity: int32 [32768], P('seq'), may hold values from 0 to 1, as said below
Outputs:
- whitened_error: bfloat16 [4, 32768, 3584], P(None, 'seq', 'feat')
- total_loss: float32 [], replicated
Inputs may be any that keep to these rules, and one draw needn't show every extreme that they name: `validity`: the positions form 2 sequences of 16384 positions each; in each sequence a prefix of 4096 positions or more is 1 and the rest is 0.
All inputs are finite; a program needn't handle non-finite values.
Results may differ from a plain program's by a relative error of at most 0.00045.
Values may be sent and summed in bfloat16 or wider, within the bound.
No kernel may reach another device: no remote copies, remote signals or barrier semaphores. Data moves between devices by JAX's collectives and lax.ppermute only.
A program may use at most 64 MiB of HBM per device.

v0:
```python
import functools

import jax
import jax.numpy as jnp
from jax import lax
from jax.sharding import Mesh
from jax.sharding import PartitionSpec as P

D = 3584
LAYERS = 4
SEQ = ("seq_0", "seq_1")
SEQ_FEAT = ("seq_0", "seq_1", "feat_0", "feat_1")
FEAT = ("feat_0", "feat_1")


epsilon = 1e-05


def all_in_one(value, axis):
    leaves = jax.tree.leaves(value)
    sequence = sorted(range(len(leaves)), key=lambda k: -leaves[k].size)
    width = (1, *leaves[sequence[0]].shape)[-1]
    lines = [
        jnp.pad(leaves[k].reshape(-1), (0, -leaves[k].size % width)).reshape(-1, width)
        for k in sequence
    ]
    both, at, found = (lax.all_gather(jnp.concatenate(lines), axis), 0, {})
    for k, line in zip(sequence, lines):
        slab = both[:, at : at + len(line)].reshape(len(both), -1)
        found[k] = slab[:, : leaves[k].size].reshape(-1, *leaves[k].shape)
        at += len(line)
    numbers = iter(range(len(leaves)))
    return jax.tree.map(lambda _: found[next(numbers)], value)


def combined_by_axis(value, axes, combine):
    for axis in axes:
        pieces = all_in_one(value, axis)
        value = jax.tree.map(lambda part: part[0], pieces)
        for k in range(1, lax.axis_size(axis)):
            value = combine(value, jax.tree.map(lambda part: part[k], pieces))
    return value


def over_axes(value, axes):
    return functools.reduce(lax.psum, axes, value)


def combine_moments(former, latter):
    first_count, first_mean, first_spread = former
    second_count, second_mean, second_spread = latter
    joined = first_count + second_count
    share = second_count / jnp.maximum(joined, 1.0)
    delta = second_mean - first_mean
    return (
        joined,
        first_mean + delta * share,
        first_spread + second_spread + delta * delta * first_count * share,
    )


def shards(teacher_states, student_states, projection, layer_pick, validity):
    all_weights = lax.all_gather(projection, SEQ, axis=1, tiled=True)
    weighting = validity.astype(jnp.float32)
    local_count = jnp.sum(weighting)
    chosen = jnp.take(teacher_states, layer_pick, axis=0).astype(jnp.float32)
    masked = weighting[None, :, None]
    local_sums = jnp.sum(chosen * masked, axis=1)
    local_mean = local_sums / jnp.maximum(local_count, 1.0)
    local_centred = chosen - local_mean[:, None, :]
    local_spread = jnp.sum(masked * local_centred * local_centred, axis=1)
    counted, average, spread = combined_by_axis(
        (local_count, local_mean, local_spread), SEQ, combine_moments
    )
    variance = spread / counted
    centred = chosen - average[:, None, :]
    target = centred / jnp.sqrt(variance + epsilon)[:, None, :]
    predicted = jnp.einsum(
        "tr,lrd->ltd", student_states, all_weights, preferred_element_type=jnp.float32
    )
    residual = predicted - target
    whitened_error = (masked * residual).astype(jnp.bfloat16)
    partial_value = jnp.sum(masked * residual * residual)
    squared_total = over_axes(partial_value, SEQ_FEAT)
    total_loss = squared_total / (counted * D * LAYERS)
    return (whitened_error, total_loss)


def solution(mesh):
    torus = Mesh(mesh.devices.reshape(8, 4, 4, 2), ("seq_0", "seq_1", "feat_0", "feat_1"))
    in_specs = (P(None, SEQ, FEAT), P(SEQ, None), P(None, SEQ, FEAT), P(), P(SEQ))
    out_specs = (P(None, SEQ, FEAT), P())
    return jax.shard_map(
        shards, mesh=torus, in_specs=in_specs, out_specs=out_specs, check_vma=False
    )
```

profile of v0, /device:TPU:1, one launch (start us, length us, event | category | flops | bytes accessed | tf_op | source)
XLA Modules:
  0.0 185.9 jit_solution(15718595818975984317)
XLA Ops:
  7.2 0.0 copy-start.1
  7.2 0.0 copy-start.2
  7.2 0.0 all-gather.6.cloned.1.call-start
  7.2 0.7 all-gather.6.cloned.1.call-update
  7.9 0.7 convert_element_type.12
  8.6 0.7 compare_select_fusion
  9.3 4.7 %gather_fusion = bf16[4,1024,448]{1,2,0:T(8,128)(2,1)} fusion(bf16[4,1024,448]{1,2,0:T(8,128)(2,1)} %param.5, s32[1024]{0:T(1024)S(1)} %pad_clamp_fusion), kind=kCustom, calls=%fused_computation | custom fusion | bytes 7340048 | tf_op jit(solution)/shard_map/jit(_take)/gather | solution.py:66
  13.9 0.0 copy-done.1
  13.9 0.6 convert_reduce_fusion
  15.2 0.0 copy-start
  15.2 0.8 pad.7
  16.0 0.0 copy-done.2
  16.0 3.3 %fusion.1 = f32[4,448]{1,0:T(4,128)S(1)} fusion(f32[1024]{0:T(1024)S(1)} %convert_element_type.12, bf16[4,1024,448]{1,2,0:T(8,128)(2,1)} %gather_fusion, pred[4]{0:T(512)(128)(4,1)S(1)} %compare_and_fusion), kind=kLoop, calls=%fused_computation.8 | loop fusion | flops 7338240 | bytes 3681284 | tf_op jit(solution)/shard_map/reduce_sum | solution.py:68
  19.4 0.0 copy-done
  19.4 1.8 fusion.4
  21.2 24.3 %all-gather.2 = f32[8,9,448]{2,1,0:T(8,128)S(1)} all-gather(f32[1,9,448]{2,1,0:T(8,128)S(1)} %maximum_bitcast_fusion), channel_id=2, replica_groups=mesh['seq_0'=8,'seq_1'=4,'feat_0'=4,'feat_1'=2] {'seq_0'}, dimensions={0}, use_global_device_ids=true | all-gather | bytes 145152 | tf_op jit(solution)/shard_map/all_gather | solution.py:27
  45.6 0.6 fusion.40
  55.8 0.7 fusion.20
  56.5 9.7 %all-gather.3 = f32[4,9,448]{2,1,0:T(8,128)S(1)} all-gather(f32[1,9,448]{2,1,0:T(8,128)S(1)} %maximum_bitcast_fusion.1), channel_id=3, replica_groups=mesh['seq_0'=8,'seq_1'=4,'feat_0'=4,'feat_1'=2] {'seq_1'}, dimensions={0}, use_global_device_ids=true | all-gather | bytes 80640 | tf_op jit(solution)/shard_map/all_gather | solution.py:27
  66.2 0.6 fusion.41
  71.3 0.7 multiply_add_fusion
  72.0 46.2 %all-gather.6.cloned.1.call-done = bf16[4,2304,448]{2,1,0:T(8,128)(2,1)} async-done(((bf16[4,72,448]{2,1,0:T(8,128)(2,1)}), bf16[4,2304,448]{2,1,0:T(8,128)(2,1)}) %all-gather.6.cloned.1.call-update) | async-done | bytes 8257552 | tf_op jit(solution)/shard_map/all_gather | solution.py:63
  118.2 19.1 %fusion = (f32[]{:T(128)}, bf16[4,1024,448]{1,2,0:T(8,128)(2,1)}) fusion(f32[1024]{0:T(1024)S(1)} %convert_element_type.12, f32[4,448]{1,0:T(4,128)S(1)} %get-tuple-element.7, f32[4,448]{1,0:T(4,128)S(1)} %get-tuple-element.6, bf16[4,1024,448]{1,2,0:T(8,128)(2,1)} %gather_fusion, pred[4]{0:T(512)(128)(4,1)S(1)} %compare_and_fusion, ...), kind=kOutput, calls=%fused_computation.7 | convolution fusion | flops 8472231936 | bytes 20334600 | tf_op jit(solution)/shard_map/tr,lrd->ltd/dot_general | solution.py:78
  137.3 13.0 %psum.28 = f32[]{:T(128)} all-reduce(f32[]{:T(128)} %get-tuple-element.4), channel_id=1, replica_groups=mesh['seq_0'=8,'seq_1'=4,'feat_0'=4,'feat_1'=2] {'seq_0'}, use_global_device_ids=true, to_apply=%region_4.5 | all-reduce | flops 1 | bytes 8 | tf_op jit(solution)/shard_map/psum | solution.py:46
  150.3 6.6 %psum.29 = f32[]{:T(128)} all-reduce(f32[]{:T(128)} %psum.28), channel_id=1, replica_groups=mesh['seq_0'=8,'seq_1'=4,'feat_0'=4,'feat_1'=2] {'seq_1'}, use_global_device_ids=true, to_apply=%region_5.6 | all-reduce | flops 1 | bytes 8 | tf_op jit(solution)/shard_map/psum | solution.py:46
  156.9 8.8 %psum.30 = f32[]{:T(128)} all-reduce(f32[]{:T(128)} %psum.29), channel_id=1, replica_groups=mesh['seq_0'=8,'seq_1'=4,'feat_0'=4,'feat_1'=2] {'feat_0'}, use_global_device_ids=true, to_apply=%region_6.7 | all-reduce | flops 1 | bytes 8 | tf_op jit(solution)/shard_map/psum | solution.py:46
  165.7 11.6 %psum.31 = f32[]{:T(128)} all-reduce(f32[]{:T(128)} %psum.30), channel_id=1, replica_groups=mesh['seq_0'=8,'seq_1'=4,'feat_0'=4,'feat_1'=2] {'feat_1'}, use_global_device_ids=true, to_apply=%region_7.8 | all-reduce | flops 1 | bytes 8 | tf_op jit(solution)/shard_map/psum | solution.py:46
  (11 shorter events, 0.1 us)
Async XLA Ops:
  7.2 6.8 %copy-start.1 = (s32[1024]{0:T(1024)S(1)}, s32[1024]{0:T(1024)}, u32[]{:S(2)}) copy-start(s32[1024]{0:T(1024)} %param.9) | copy-start | bytes 12292
  7.2 8.8 %copy-start.2 = (s32[4]{0:T(128)S(1)}, s32[4]{0:T(128)}, u32[]{:S(2)}) copy-start(s32[4]{0:T(128)} %param.8) | copy-start | bytes 52
  7.2 111.0 %all-gather.6.cloned.1.call-start = ((), (), s32[]{:S(2)}) async-start(), calls=%async_computation | async-start | bytes 9732096 | tf_op jit(solution)/shard_map/all_gather | solution.py:63
  15.2 4.2 %copy-start = (bf16[4,1024,448]{1,2,0:T(8,128)(2,1)S(1)}, bf16[4,1024,448]{1,2,0:T(8,128)(2,1)}, u32[]{:S(2)}) copy-start(bf16[4,1024,448]{1,2,0:T(8,128)(2,1)} %gather_fusion) | copy-start | bytes 11010052
Sparse Core Ops, SparseCore 0:
  10.6 107.5 all-gather.5
where the time goes:
time: 186 us
  blocking collectives  74.1 us (40%)
  waiting for transfers between devices  46.9 us (25%)
  between operations  30.6 us (16%)
  matrix products  19.1 us (10%)
  other arithmetic  8.52 us (5%)
  local copies, waits for them, and re-layouts  6.71 us (4%)
    all_gather x1, waiting for transfers between devices, shards(): all_weights = lax.all_gather(projection, SEQ, axis=1, tiled=True)  46.2 us
    psum x4, blocking collectives, over_axes(): return functools.reduce(lax.psum, axes, value)  40 us
    all_gather x2, blocking collectives, all_in_one(): both, at, found = (lax.all_gather(jnp.concatenate(lines), axis), 0, {})  34 us
    dot_general x1, matrix products, shards(): jnp.einsum('tr,lrd->ltd', student_states, all_weights, preferred_element_...  19.1 us
    gather x1, local copies, waits for them, and re-layouts, shards(): chosen = jnp.take(teacher_states, layer_pick, axis=0).astype(jnp.float32)  4.65 us
  transfers between devices with their start and end apart: 1, of which 1 were waited for; matrix products, arithmetic and copies ran while one was open for 8% of the time, Pallas kernels for 0%

commit v1 on v0

v1 whole, which is shorter than its diff:
```python
import jax
import jax.numpy as jnp
from jax import lax
from jax.experimental import pallas as pl
from jax.experimental.pallas import tpu as pltpu
from jax.sharding import Mesh
from jax.sharding import PartitionSpec as P

D = 3584
LAYERS = 4
SEQ = ("seq_0", "seq_1")
FEAT = ("feat_0", "feat_1")
ALL = SEQ + FEAT
NZ, NX = 8, 4
epsilon = 1e-05

C_COLS = 768
HALF = 512
BN = 256
VMEM = 56 * 1024 * 1024

Z_ORDER = (0, 1, -1, 2, -2, 3, -3, 4)
X_ORDER = (0, 1, -1, 2)
NEAR = 3
f32 = jnp.float32
bf16 = jnp.bfloat16


def shift(value, axis, size, by):
    return lax.ppermute(value, axis, [(i, (i - by) % size) for i in range(size)])


def from_z(value, by):
    return shift(value, "seq_0", NZ, by)


def from_x(value, by):
    return shift(value, "seq_1", NX, by)


def params(**kw):
    return pltpu.CompilerParams(vmem_limit_bytes=VMEM, **kw)


def moments_kernel(pick, teacher, weight, chosen, stats):
    x16 = teacher[0]
    chosen[0] = x16
    x = x16.astype(f32)
    w = weight[...]
    count = jnp.sum(w, axis=1, keepdims=True)
    mean = jnp.sum(x * w, axis=1, keepdims=True) / jnp.maximum(count, 1.0)
    centred = x - mean
    spread = jnp.sum(w * centred * centred, axis=1, keepdims=True)
    lane = lax.broadcasted_iota(jnp.int32, (x.shape[0], 128), 1)
    table = jnp.where(lane == 0, mean, jnp.where(lane == 1, spread, count))
    stats[0] = table.T[:8]


def local_moments(teacher, weight, pick):
    layers, features, tokens = teacher.shape
    return pl.pallas_call(
        moments_kernel,
        grid_spec=pltpu.PrefetchScalarGridSpec(
            num_scalar_prefetch=1,
            grid=(layers,),
            in_specs=[
                pl.BlockSpec((1, features, tokens), lambda i, p: (p[i], 0, 0)),
                pl.BlockSpec((1, tokens), lambda i, p: (0, 0)),
            ],
            out_specs=[
                pl.BlockSpec((1, features, tokens), lambda i, p: (i, 0, 0)),
                pl.BlockSpec((1, 8, features), lambda i, p: (i, 0, 0)),
            ],
        ),
        out_shape=[
            jax.ShapeDtypeStruct((layers, features, tokens), bf16),
            jax.ShapeDtypeStruct((layers, 8, features), f32),
        ],
        compiler_params=params(),
        cost_estimate=pl.CostEstimate(flops=20_000_000, bytes_accessed=8_000_000, transcendentals=0),
        name="moments",
    )(pick, teacher, weight)


def merge(former, latter):
    first_mean, first_spread, first_count = former[:, 0], former[:, 1], former[:, 2]
    second_mean, second_spread, second_count = latter[:, 0], latter[:, 1], latter[:, 2]
    joined = first_count + second_count
    share = second_count / jnp.maximum(joined, 1.0)
    delta = second_mean - first_mean
    mean = first_mean + delta * share
    spread = first_spread + second_spread + delta * delta * first_count * share
    row = lax.broadcasted_iota(jnp.int32, former.shape, 1)
    return jnp.where(row == 0, mean[:, None], jnp.where(row == 1, spread[:, None], joined[:, None]))


def order_kernel(zs, xs, student, near, far):
    i = pl.program_id(0)

    @pl.when(i < NEAR)
    def _():
        for j in range(NX):
            near[j, 0] = student[0, xs[j]]

    @pl.when(i >= NEAR)
    def _():
        for j in range(NX):
            far[j, 0] = student[0, xs[j]]


def in_order(student, zs, xs):
    nz, nx, rows, tokens = student.shape
    return pl.pallas_call(
        order_kernel,
        grid_spec=pltpu.PrefetchScalarGridSpec(
            num_scalar_prefetch=2,
            grid=(nz,),
            in_specs=[pl.BlockSpec((1, nx, rows, tokens), lambda i, z, x: (z[i], 0, 0, 0))],
            out_specs=[
                pl.BlockSpec((nx, 1, rows, tokens), lambda i, z, x: (0, jnp.minimum(i, NEAR - 1), 0, 0)),
                pl.BlockSpec((nx, 1, rows, tokens), lambda i, z, x: (0, jnp.maximum(i - NEAR, 0), 0, 0)),
            ],
        ),
        out_shape=[
            jax.ShapeDtypeStruct((nx, NEAR, rows, tokens), bf16),
            jax.ShapeDtypeStruct((nx, nz - NEAR, rows, tokens), bf16),
        ],
        compiler_params=params(),
        cost_estimate=pl.CostEstimate(flops=0, bytes_accessed=10_000_000, transcendentals=0),
        name="student_order",
    )(zs, xs, student)


def times(weights, student):
    return lax.dot_general(weights, student, (((0,), (0,)), ((), ())), preferred_element_type=f32)


def finish(predicted, chosen, scale, weight, error):
    target = (chosen[...].astype(f32) - scale[:, 0:1]) * scale[:, 1:2]
    residual = predicted - target
    masked = weight[...] * residual
    error[...] = masked.astype(bf16)
    return jnp.sum(masked * residual, axis=0, keepdims=True)


def whole_kernel(weights, student, chosen, scale, weight, error, loss):
    @pl.when(pl.program_id(0) == 0)
    def _():
        loss[...] = jnp.zeros_like(loss)

    loss[...] += finish(times(weights[...], student[...]), chosen, scale, weight, error)


def whole_product(weights, student, chosen, scale, weight):
    k, cols = weights.shape
    rows, tokens = chosen.shape
    return pl.pallas_call(
        whole_kernel,
        grid=(cols // BN,),
        in_specs=[
            pl.BlockSpec((k, BN), lambda i: (0, i)),
            pl.BlockSpec((k, tokens), lambda i: (0, 0)),
            pl.BlockSpec((BN, tokens), lambda i: (i, 0)),
            pl.BlockSpec((BN, 2), lambda i: (i, 0)),
            pl.BlockSpec((1, tokens), lambda i: (0, 0)),
        ],
        out_specs=[
            pl.BlockSpec((BN, tokens), lambda i: (i, 0)),
            pl.BlockSpec((1, tokens), lambda i: (0, 0)),
        ],
        out_shape=[
            jax.ShapeDtypeStruct((rows, tokens), bf16),
            jax.ShapeDtypeStruct((1, tokens), f32),
        ],
        compiler_params=params(),
        cost_estimate=pl.CostEstimate(flops=2 * k * cols * tokens, bytes_accessed=14_000_000, transcendentals=0),
        name="whole_product",
    )(weights, student, chosen, scale, weight)


def part_kernel(n, has_total, *refs):
    total = refs[-1]
    acc = refs[2 * n][...] if has_total else None
    for k in range(n):
        term = times(refs[k][...], refs[n + k][0])
        acc = term if acc is None else acc + term
    total[...] = acc


def part_product(weights, students, total=None):
    n = len(weights)
    cols = weights[0].shape[1]
    tokens = students[0][0].shape[2]
    in_specs = [pl.BlockSpec((w.shape[0], BN), lambda i: (0, i)) for w in weights]
    in_specs += [pl.BlockSpec((1, *s.shape[1:]), lambda i, j=j: (j, 0, 0)) for s, j in students]
    args = list(weights) + [s for s, _ in students]
    if total is not None:
        in_specs.append(pl.BlockSpec((BN, tokens), lambda i: (i, 0)))
        args.append(total)
    depth = sum(w.shape[0] for w in weights)
    return pl.pallas_call(
        lambda *refs: part_kernel(n, total is not None, *refs),
        grid=(cols // BN,),
        in_specs=in_specs,
        out_specs=pl.BlockSpec((BN, tokens), lambda i: (i, 0)),
        out_shape=jax.ShapeDtypeStruct((cols, tokens), f32),
        input_output_aliases={} if total is None else {len(args) - 1: 0},
        compiler_params=params(),
        cost_estimate=pl.CostEstimate(flops=2 * depth * cols * tokens, bytes_accessed=12_000_000, transcendentals=0),
        name="part_product",
    )(*args)


def last_kernel(left_blocks, steps, left, right, student, total, chosen, scale, weight, loss_in, error_in, error, loss, sums):
    i = pl.program_id(0)

    @pl.when(i == 0)
    def _():
        sums[...] = loss_in[...]

    weights = jnp.where(i < left_blocks, left[...], right[...])
    predicted = total[...] + times(weights, student[0])
    sums[...] += finish(predicted, chosen, scale, weight, error)

    @pl.when(i == steps - 1)
    def _():
        loss[...] = jnp.broadcast_to(jnp.sum(sums[...], axis=1, keepdims=True), loss.shape)


def last_product(left, right, student, index, total, chosen, scale, weight, loss_in, error_in, copies):
    k, tokens = student.shape[1:]
    lefts, rights = left.shape[1] // BN, right.shape[1] // BN
    first = C_COLS // BN
    steps = lefts + rights
    return pl.pallas_call(
        lambda *refs: last_kernel(lefts, steps, *refs),
        grid=(steps,),
        in_specs=[
            pl.BlockSpec((k, BN), lambda i: (0, jnp.minimum(i, lefts - 1))),
            pl.BlockSpec((k, BN), lambda i: (0, jnp.maximum(i - lefts, 0))),
            pl.BlockSpec((1, k, tokens), lambda i: (index, 0, 0)),
            pl.BlockSpec((BN, tokens), lambda i: (i, 0)),
            pl.BlockSpec((BN, tokens), lambda i: (i + first, 0)),
            pl.BlockSpec((BN, 2), lambda i: (i + first, 0)),
            pl.BlockSpec((1, tokens), lambda i: (0, 0)),
            pl.BlockSpec((1, tokens), lambda i: (0, 0)),
            pl.BlockSpec(memory_space=pl.ANY),
        ],
        out_specs=[
            pl.BlockSpec((BN, tokens), lambda i: (i + first, 0)),
            pl.BlockSpec((copies, 128), lambda i: (0, 0)),
        ],
        out_shape=[
            jax.ShapeDtypeStruct(error_in.shape, bf16),
            jax.ShapeDtypeStruct((copies, 128), f32),
        ],
        scratch_shapes=[pltpu.VMEM((1, tokens), f32)],
        input_output_aliases={8: 0},
        compiler_params=params(),
        cost_estimate=pl.CostEstimate(flops=2 * k * steps * BN * tokens, bytes_accessed=12_000_000, transcendentals=0),
        name="last_product",
    )(left, right, student, total, chosen, scale, weight, loss_in, error_in)


def shards(teacher_states, student_states, projection, layer_pick, validity):
    z, x = lax.axis_index("seq_0"), lax.axis_index("seq_1")
    layers, rows, features = projection.shape
    tokens, depth = student_states.shape
    columns = layers * features

    mine = jnp.transpose(projection, (1, 0, 2)).reshape(rows, columns)
    c_mine, b_mine = mine[:, :C_COLS], mine[:, C_COLS:]

    c_next, c_last, c_far = from_x(c_mine, 1), from_x(c_mine, -1), from_x(c_mine, 2)
    ring = {0: b_mine}
    for step in range(1, NZ // 2):
        ring[step] = from_z(ring[step - 1], 1)
        ring[-step] = from_z(ring[1 - step], -1)
    ring[NZ // 2] = from_z(ring[NZ // 2 - 1], 1)

    place = lax.broadcasted_iota(jnp.int32, (NX, 1, 1), 0)
    away = (place - x) % NX
    c_block = jnp.where(
        away == 0, c_mine[None], jnp.where(away == 1, c_next[None], jnp.where(away == 2, c_far[None], c_last[None]))
    ).reshape(NX * rows, C_COLS)
    c_weights = lax.all_gather(c_block, "seq_0", axis=0, tiled=True)

    near = jnp.concatenate([ring[k] for k in Z_ORDER[:NEAR]])
    far = jnp.concatenate([ring[k] for k in Z_ORDER[NEAR:]])

    def along_x(block):
        after, before = from_x(block, 1), from_x(block, -1)
        left, right = from_x(after[:, :HALF], 1), from_x(before[:, HALF:], -1)
        return after, before, left, right

    near_after, near_before, near_left, near_right = along_x(near)
    far_after, far_before, far_left, far_right = along_x(far)

    weight = validity.astype(f32).reshape(1, tokens)
    chosen, stats = local_moments(jnp.transpose(teacher_states, (0, 2, 1)), weight, layer_pick)
    for axis, size in (("seq_1", NX), ("seq_0", NZ)):
        step = 1
        while step < size:
            stats = merge(stats, shift(stats, axis, size, step))
            step *= 2
    counted = stats[0, 2, 0]
    scale = jnp.stack(
        [stats[:, 0].reshape(columns), (1.0 / jnp.sqrt(stats[:, 1] / stats[:, 2] + epsilon)).reshape(columns)], axis=1
    )
    chosen = chosen.reshape(columns, tokens)

    student = student_states.T
    zs = (z + jnp.asarray(Z_ORDER, jnp.int32)) % NZ
    xs = (x + jnp.asarray(X_ORDER, jnp.int32)) % NX
    s_near, s_far = in_order(student.reshape(NZ, NX, rows, tokens), zs, xs)
    s_near, s_far = s_near.reshape(NX, -1, tokens), s_far.reshape(NX, -1, tokens)

    near_across = jnp.concatenate([near_left, near_right], axis=1)
    total = part_product(
        [near, near_after, near_before, near_across, far],
        [(s_near, 0), (s_near, 1), (s_near, 2), (s_near, 3), (s_far, 0)],
    )
    total = part_product([far_after, far_before], [(s_far, 1), (s_far, 2)], total)
    error, loss = whole_product(c_weights, student, chosen, scale, weight)
    copies = NZ * NX * lax.axis_size("feat_0") * lax.axis_size("feat_1")
    error, loss = last_product(
        far_left, far_right, s_far, 3, total, chosen, scale, weight, loss, error, copies
    )
    squares = jnp.sum(lax.all_to_all(loss, ALL, 0, 0, tiled=True)[:, 0])
    total_loss = squares / (counted * D * LAYERS)
    whitened = jnp.transpose(error.reshape(layers, features, tokens), (0, 2, 1))
    return whitened, total_loss


def solution(mesh):
    torus = Mesh(mesh.devices.reshape(NZ, NX, 4, 2), ALL)
    in_specs = (P(None, SEQ, FEAT), P(SEQ, None), P(None, SEQ, FEAT), P(), P(SEQ))
    out_specs = (P(None, SEQ, FEAT), P())
    return jax.shard_map(shards, mesh=torus, in_specs=in_specs, out_specs=out_specs, check_vma=False)
```

time: 186 us -> 186 us (level)
  blocking collectives: 74.1 us -> 0 us
  starting transfers between devices: 0.04 us -> 52.6 us
  Pallas kernels: 0 us -> 43.4 us
  matrix products: 19.1 us -> 0 us
  between operations: 30.6 us -> 16.9 us
  local copies, waits for them, and re-layouts: 6.71 us -> 15.6 us
    all_gather x1, waiting for transfers between devices: 46.2 us -> 0.01 us  [shards(): c_weights = lax.all_gather(c_block, 'seq_0', axis=0, tiled=True)]
    pallas_call x0 -> x6, Pallas kernels: none -> 43.4 us  [the longest x2 15 us: part_product(): pl.pallas_call(lambda *refs: part_kernel(n, total is not None, *refs), gr...]
    psum x4 -> x0, blocking collectives: 40 us -> none  [over_axes(): return functools.reduce(lax.psum, axes, value)]
    ppermute x0 -> x23, starting transfers between devices: none -> 36.5 us  [shift(): lax.ppermute(value, axis, [(i, (i - by) % size) for i in range(size)])]
    ppermute x0 -> x23, waiting for transfers between devices: none -> 35.9 us  [shift(): lax.ppermute(value, axis, [(i, (i - by) % size) for i in range(size)])]
    all_gather x2 -> x0, blocking collectives: 34 us -> none  [all_in_one(): both, at, found = (lax.all_gather(jnp.concatenate(lines), axis), 0, {})]
    dot_general x1 -> x0, matrix products: 19.1 us -> none  [shards(): jnp.einsum('tr,lrd->ltd', student_states, all_weights, preferred_element_...]
    all_to_all x0 -> x1, starting transfers between devices: none -> 16.1 us  [shards(): squares = jnp.sum(lax.all_to_all(loss, ALL, 0, 0, tiled=True)[:, 0])]
  transfers between devices with their start and end apart: 1 -> 25, of which waited for: 1 -> 13; matrix products, arithmetic and copies ran while one was open for 8% -> 11% of each run, Pallas kernels for 0% -> 20%
where the time goes in v1:
time: 186 us; the launch traced here: 185 us
  starting transfers between devices  52.6 us (28%)
  waiting for transfers between devices  47.1 us (25%)
  Pallas kernels  43.4 us (23%)
  between operations  16.9 us (9%)
  local copies, waits for them, and re-layouts  15.6 us (8%)
  other arithmetic  9.26 us (5%)
    ppermute x23, starting transfers between devices, shift(): lax.ppermute(value, axis, [(i, (i - by) % size) for i in range(size)])  36.5 us
    ppermute x23, waiting for transfers between devices, shift(): lax.ppermute(value, axis, [(i, (i - by) % size) for i in range(size)])  35.9 us
    all_to_all x1, starting transfers between devices, shards(): squares = jnp.sum(lax.all_to_all(loss, ALL, 0, 0, tiled=True)[:, 0])  16.1 us
    pallas_call x2, Pallas kernels, part_product(): pl.pallas_call(lambda *refs: part_kernel(n, total is not None, *refs), gr...  15 us
    all_to_all x1, waiting for transfers between devices, shards(): squares = jnp.sum(lax.all_to_all(loss, ALL, 0, 0, tiled=True)[:, 0])  11.1 us
    pallas_call x1, Pallas kernels, whole_product(): pl.pallas_call(whole_kernel, grid=(cols // BN,), in_specs=[pl.BlockSpec((...  8.45 us
    unnamed x41, local copies, waits for them, and re-layouts  8.26 us
    pallas_call x1, Pallas kernels, in_order(): pl.pallas_call(order_kernel, grid_spec=pltpu.PrefetchScalarGridSpec(num_s...  7.57 us
  transfers between devices with their start and end apart: 25, of which 13 were waited for; matrix products, arithmetic and copies ran while one was open for 11% of the time, Pallas kernels for 20%

profile of v1, /device:TPU:1, one launch (start us, length us, event | category | flops | bytes accessed | tf_op | source)
XLA Modules:
  0.0 184.8 jit_solution(14921680710159196161)
XLA Ops:
  7.2 1.1 copy.17
  8.7 3.4 %collective-permute-start.20 = (bf16[72,768]{1,0:T(8,128)(2,1)S(1)}, bf16[72,768]{1,0:T(8,128)(2,1)S(1)}, u32[]{:S(2)}, u32[]{:S(2)}) collective-permute-start(bf16[72,768]{1,0:T(8,128)(2,1)S(1)} %slice.199), channel_id=1, source_target_pairs={{0,24},{8,0},{16,8},{24,16},{1,25},{9,1},{17,9},{25,17},{2,26},{10... | collective-permute-start | bytes 331784 | tf_op jit(solution)/shard_map/ppermute | solution.py:30
  13.7 1.0 collective-permute-done.20
  14.7 2.5 %collective-permute-done.21 = bf16[72,768]{1,0:T(8,128)(2,1)S(1)} collective-permute-done((bf16[72,768]{1,0:T(8,128)(2,1)S(1)}, bf16[72,768]{1,0:T(8,128)(2,1)S(1)}, u32[]{:S(2)}, u32[]{:S(2)}) %collective-permute-start.21) | collective-permute-done | bytes 110624 | tf_op jit(solution)/shard_map/ppermute | solution.py:30
  17.3 3.2 %collective-permute-done.22 = bf16[72,768]{1,0:T(8,128)(2,1)S(1)} collective-permute-done((bf16[72,768]{1,0:T(8,128)(2,1)S(1)}, bf16[72,768]{1,0:T(8,128)(2,1)S(1)}, u32[]{:S(2)}, u32[]{:S(2)}) %collective-permute-start.22) | collective-permute-done | bytes 110624 | tf_op jit(solution)/shard_map/ppermute | solution.py:30
  20.4 1.0 fusion.1
  21.4 1.3 convert_element_type.3
  22.7 5.9 %moments.1 = (bf16[4,448,1024]{2,1,0:T(8,128)(2,1)}, f32[4,8,448]{2,1,0:T(8,128)}) custom-call(s32[4]{0:T(128)} %pick.1, bf16[4,448,1024]{2,1,0:T(8,128)(2,1)} %bitcast.82, f32[1,1024]{1,0:T(1,128)} %bitcast.89), custom_call_target="tpu_custom_call" | custom-call | flops 20000000 | bytes 8000000 | tf_op jit(solution)/shard_map/moments/pallas_call | solution.py:61
  28.6 3.3 %collective-permute-done.15 = f32[4,8,448]{2,1,0:T(8,128)S(1)} collective-permute-done((f32[4,8,448]{2,1,0:T(8,128)}, f32[4,8,448]{2,1,0:T(8,128)S(1)}, u32[]{:S(2)}, u32[]{:S(2)}) %collective-permute-start.15) | collective-permute-done | bytes 57376 | tf_op jit(solution)/shard_map/ppermute | solution.py:30
  31.9 0.9 multiply_add_fusion.4
  32.9 1.0 fusion.6
  34.2 5.7 %collective-permute-start = (bf16[72,1024]{1,0:T(8,128)(2,1)S(1)}, bf16[72,1024]{1,0:T(8,128)(2,1)S(1)}, u32[]{:S(2)}, u32[]{:S(2)}) collective-permute-start(bf16[72,1024]{1,0:T(8,128)(2,1)S(1)} %slice.164), channel_id=1, source_target_pairs={{0,224},{32,0},{64,32},{96,64},{128,96},{160,128},{192,160},{224,1... | collective-permute-start | bytes 442376 | tf_op jit(solution)/shard_map/ppermute | solution.py:30
  40.1 4.5 %collective-permute-start.17 = (f32[4,8,448]{2,1,0:T(8,128)S(1)}, f32[4,8,448]{2,1,0:T(8,128)S(1)}, u32[]{:S(2)}, u32[]{:S(2)}) collective-permute-start(f32[4,8,448]{2,1,0:T(8,128)S(1)} %select_select_fusion.3), channel_id=1, source_target_pairs={{0,224},{32,0},{64,32},{96,64},{128,96},{160,128},{192,160},{224,1... | collective-permute-start | bytes 172040 | tf_op jit(solution)/shard_map/ppermute | solution.py:30
  45.1 2.7 %collective-permute-done.17 = f32[4,8,448]{2,1,0:T(8,128)S(1)} collective-permute-done((f32[4,8,448]{2,1,0:T(8,128)S(1)}, f32[4,8,448]{2,1,0:T(8,128)S(1)}, u32[]{:S(2)}, u32[]{:S(2)}) %collective-permute-start.17) | collective-permute-done | bytes 57376 | tf_op jit(solution)/shard_map/ppermute | solution.py:30
  48.0 3.4 %collective-permute-start.18 = (f32[4,8,448]{2,1,0:T(8,128)S(1)}, f32[4,8,448]{2,1,0:T(8,128)S(1)}, u32[]{:S(2)}, u32[]{:S(2)}) collective-permute-start(f32[4,8,448]{2,1,0:T(8,128)S(1)} %select_select_fusion.2), channel_id=1, source_target_pairs={{0,192},{32,224},{64,0},{96,32},{128,64},{160,96},{192,128},{224,1... | collective-permute-start | bytes 172040 | tf_op jit(solution)/shard_map/ppermute | solution.py:30
  51.9 6.6 %copy.18 = bf16[1024,2304]{0,1:T(8,128)(2,1)} copy(bf16[1024,2304]{1,0:T(8,128)(2,1)} %param.8) | data formatting | bytes 9437184 | tf_op args[1]
  58.6 7.6 %student_order.1 = (bf16[4,3,72,1024]{3,2,1,0:T(8,128)(2,1)}, bf16[4,5,72,1024]{3,2,1,0:T(8,128)(2,1)}) custom-call(s32[8]{0:T(128)} %and_select_fusion.2.zs, s32[4]{0:T(128)} %and_select_fusion.1.xs, bf16[8,4,72,1024]{3,2,1,0:T(8,128)(2,1)} %bitcast.80), custom_call_target="tpu_custom_call" | custom-call | bytes 10000000 | tf_op jit(solution)/shard_map/student_order/pallas_call | solution.py:113
  66.3 1.0 collective-permute-start.19
  67.4 2.3 %collective-permute-start.11 = (bf16[216,1024]{1,0:T(8,128)(2,1)S(1)}, bf16[216,1024]{1,0:T(8,128)(2,1)S(1)}, u32[]{:S(2)}, u32[]{:S(2)}) collective-permute-start(bf16[216,1024]{1,0:T(8,128)(2,1)S(1)} %pad_maximum_fusion.refs_0_), channel_id=1, source_target_pairs={{0,24},{8,0},{16,8},{24,16},{1,25},{9,1},{17,9},{25,17},{2,26},{10... | collective-permute-start | bytes 1327112 | tf_op jit(solution)/shard_map/ppermute | solution.py:30
  69.7 1.2 collective-permute-start.1
  70.9 1.2 collective-permute-start.3
  72.0 3.0 %collective-permute-done.19 = f32[4,8,448]{2,1,0:T(8,128)S(1)} collective-permute-done((f32[4,8,448]{2,1,0:T(8,128)S(1)}, f32[4,8,448]{2,1,0:T(8,128)S(1)}, u32[]{:S(2)}, u32[]{:S(2)}) %collective-permute-start.19) | collective-permute-done | bytes 57376 | tf_op jit(solution)/shard_map/ppermute | solution.py:30
  75.1 5.2 %collective-permute-done.1 = bf16[72,1024]{1,0:T(8,128)(2,1)S(1)} collective-permute-done((bf16[72,1024]{1,0:T(8,128)(2,1)S(1)}, bf16[72,1024]{1,0:T(8,128)(2,1)S(1)}, u32[]{:S(2)}, u32[]{:S(2)}) %collective-permute-start.1) | collective-permute-done | bytes 147488 | tf_op jit(solution)/shard_map/ppermute | solution.py:30
  80.4 1.9 %collective-permute-start.4 = (bf16[72,1024]{1,0:T(8,128)(2,1)S(1)}, bf16[72,1024]{1,0:T(8,128)(2,1)S(1)}, u32[]{:S(2)}, u32[]{:S(2)}) collective-permute-start(bf16[72,1024]{1,0:T(8,128)(2,1)S(1)} %collective-permute-done.1), channel_id=1, source_target_pairs={{0,224},{32,0},{64,32},{96,64},{128,96},{160,128},{192,160},{224,1... | collective-permute-start | bytes 442376 | tf_op jit(solution)/shard_map/ppermute | solution.py:30
  82.4 2.3 %collective-permute-done.4 = bf16[72,1024]{1,0:T(8,128)(2,1)S(1)} collective-permute-done((bf16[72,1024]{1,0:T(8,128)(2,1)S(1)}, bf16[72,1024]{1,0:T(8,128)(2,1)S(1)}, u32[]{:S(2)}, u32[]{:S(2)}) %collective-permute-start.4) | collective-permute-done | bytes 147488 | tf_op jit(solution)/shard_map/ppermute | solution.py:30
  84.7 2.7 %collective-permute-start.6 = (bf16[72,1024]{1,0:T(8,128)(2,1)S(1)}, bf16[72,1024]{1,0:T(8,128)(2,1)S(1)}, u32[]{:S(2)}, u32[]{:S(2)}) collective-permute-start(bf16[72,1024]{1,0:T(8,128)(2,1)S(1)} %collective-permute-done.4), channel_id=1, source_target_pairs={{0,224},{32,0},{64,32},{96,64},{128,96},{160,128},{192,160},{224,1... | collective-permute-start | bytes 442376 | tf_op jit(solution)/shard_map/ppermute | solution.py:30
  87.5 2.0 %collective-permute-done.6 = bf16[72,1024]{1,0:T(8,128)(2,1)S(1)} collective-permute-done((bf16[72,1024]{1,0:T(8,128)(2,1)S(1)}, bf16[72,1024]{1,0:T(8,128)(2,1)S(1)}, u32[]{:S(2)}, u32[]{:S(2)}) %collective-permute-start.6) | collective-permute-done | bytes 147488 | tf_op jit(solution)/shard_map/ppermute | solution.py:30
  89.6 2.4 %collective-permute-start.7 = (bf16[360,1024]{1,0:T(8,128)(2,1)S(1)}, bf16[360,1024]{1,0:T(8,128)(2,1)S(1)}, u32[]{:S(2)}, u32[]{:S(2)}) collective-permute-start(bf16[360,1024]{1,0:T(8,128)(2,1)S(1)} %constant_dynamic-update-slice_fusion.refs_4_), channel_id=1, source_target_pairs={{0,24},{8,0},{16,8},{24,16},{1,25},{9,1},{17,9},{25,17},{2,26},{10... | collective-permute-start | bytes 2211848 | tf_op jit(solution)/shard_map/ppermute | solution.py:30
  92.8 0.7 sqrt.6
  93.5 0.7 stack_reshape_squeeze.3
  94.1 0.8 slice.167
  94.9 2.7 %collective-permute-start.13 = (bf16[216,512]{1,0:T(8,128)(2,1)}, bf16[216,512]{1,0:T(8,128)(2,1)}, u32[]{:S(2)}, u32[]{:S(2)}) collective-permute-start(bf16[216,512]{1,0:T(8,128)(2,1)} %slice.167), channel_id=1, source_target_pairs={{0,24},{8,0},{16,8},{24,16},{1,25},{9,1},{17,9},{25,17},{2,26},{10... | collective-permute-start | bytes 663560 | tf_op jit(solution)/shard_map/ppermute | solution.py:30
  97.6 0.7 slice.168
  98.4 0.7 pad_maximum_fusion.2
  99.1 1.3 copy.20.scale.refs_5_
  100.4 7.5 %collective-permute-done.13 = bf16[216,512]{1,0:T(8,128)(2,1)} collective-permute-done((bf16[216,512]{1,0:T(8,128)(2,1)}, bf16[216,512]{1,0:T(8,128)(2,1)}, u32[]{:S(2)}, u32[]{:S(2)}) %collective-permute-start.13) | collective-permute-done | bytes 221216 | tf_op jit(solution)/shard_map/ppermute | solution.py:30
  107.8 3.0 %collective-permute-done.14 = bf16[216,512]{1,0:T(8,128)(2,1)} collective-permute-done((bf16[216,512]{1,0:T(8,128)(2,1)}, bf16[216,512]{1,0:T(8,128)(2,1)}, u32[]{:S(2)}, u32[]{:S(2)}) %collective-permute-start.14) | collective-permute-done | bytes 221216 | tf_op jit(solution)/shard_map/ppermute | solution.py:30
  110.8 1.9 %pad_maximum_fusion.1.refs_3_ = bf16[216,1024]{1,0:T(8,128)(2,1)} fusion(bf16[216,512]{1,0:T(8,128)(2,1)} %collective-permute-done.14, bf16[216,512]{1,0:T(8,128)(2,1)} %collective-permute-done.13), kind=kLoop, calls=%fused_computation.1 | loop fusion | flops 884736 | bytes 884736 | tf_op jit(solution)/shard_map/concatenate | solution.py:318
  112.7 7.7 %part_product.2.refs_4_ = f32[1024,1024]{1,0:T(8,128)} custom-call(bf16[216,1024]{1,0:T(8,128)(2,1)} %copy-done, bf16[216,1024]{1,0:T(8,128)(2,1)} %copy-done.4, bf16[216,1024]{1,0:T(8,128)(2,1)} %copy-done.5, bf16[216,1024]{1,0:T(8,128)(2,1)} %pad_maximum_fusion.1.refs_3_, bf16[360,1024]{1,0:T(8,128)(2,1)} %copy-done.3, bf16[4,216,1024]{2,1,0:T(8,128)(2,1)} %bitcast.76, ...), custom_call_target="tpu_custom_call" | custom-call | flops 2566914048 | bytes 12000000 | tf_op jit(solution)/shard_map/part_product/pallas_call | solution.py:201
  120.7 2.7 %collective-permute-start.8 = (bf16[360,512]{1,0:T(8,128)(2,1)S(1)}, bf16[360,512]{1,0:T(8,128)(2,1)S(1)}, u32[]{:S(2)}, u32[]{:S(2)}) collective-permute-start(bf16[360,512]{1,0:T(8,128)(2,1)S(1)} %slice.165), channel_id=1, source_target_pairs={{0,24},{8,0},{16,8},{24,16},{1,25},{9,1},{17,9},{25,17},{2,26},{10... | collective-permute-start | bytes 1105928 | tf_op jit(solution)/shard_map/ppermute | solution.py:30
  123.4 7.3 %part_product.3.refs_3_ = f32[1024,1024]{1,0:T(8,128)} custom-call(bf16[360,1024]{1,0:T(8,128)(2,1)} %copy-done.1, bf16[360,1024]{1,0:T(8,128)(2,1)} %copy-done.2, bf16[4,360,1024]{2,1,0:T(8,128)(2,1)} %bitcast.73, bf16[4,360,1024]{2,1,0:T(8,128)(2,1)} %bitcast.74, f32[1024,1024]{1,0:T(8,128)} %part_product.2.refs_4_), custom_call_target="tpu_custom_call", output_to_operand_aliasing={{}: (4, {})} | custom-call | flops 1509949440 | bytes 12000000 | tf_op jit(solution)/shard_map/part_product/pallas_call | solution.py:201
  130.7 8.4 %whole_product.1 = (bf16[1792,1024]{1,0:T(8,128)(2,1)}, f32[1,1024]{1,0:T(1,128)}) custom-call(bf16[2304,768]{1,0:T(8,128)(2,1)} %all-gather.2.cloned.1.call-done.weights, bf16[2304,1024]{1,0:T(8,128)(2,1)} %bitcast.81, bf16[1792,1024]{1,0:T(8,128)(2,1)} %bitcast.83, f32[1792,2]{1,0:T(8,128)} %copy.20.scale.refs_5_, f32[1,1024]{1,0:T(1,128)} %bitcast.90), custom_call_target="tpu_custom_call" | custom-call | flops 3623878656 | bytes 14000000 | tf_op jit(solution)/shard_map/whole_product/pallas_call | solution.py:157
  139.2 0.7 copy-done.6
  140.0 6.4 %last_product.1 = (bf16[1792,1024]{1,0:T(8,128)(2,1)}, f32[256,128]{1,0:T(8,128)}) custom-call(bf16[360,512]{1,0:T(8,128)(2,1)} %copy-done.7, bf16[360,512]{1,0:T(8,128)(2,1)} %copy-done.6, bf16[4,360,1024]{2,1,0:T(8,128)(2,1)} %bitcast.75, f32[1024,1024]{1,0:T(8,128)} %part_product.3.refs_3_, ...), custom_call_target="tpu_custom_call", output_to_operand_aliasing={{0}: (8, {})} | custom-call | flops 754974720 | bytes 12000000 | tf_op jit(solution)/shard_map/last_product/pallas_call | solution.py:235
  146.4 16.1 %all-to-all-start = ((f32[256,1,128]{2,1,0:T(1,128)}), f32[256,1,128]{2,1,0:T(1,128)S(1)}, u32[]{:S(2)}, u32[]{:S(2)}) async-start(f32[256,1,128]{2,1,0:T(1,128)} %bitcast.88), calls=%async_computation | async-start | bytes 262144 | tf_op jit(solution)/shard_map/all_to_all | solution.py:329
  162.5 1.2 slice.201
  164.4 11.1 %all-to-all-done = f32[256,1,128]{2,1,0:T(1,128)S(1)} async-done(((f32[256,1,128]{2,1,0:T(1,128)}), f32[256,1,128]{2,1,0:T(1,128)S(1)}, u32[]{:S(2)}, u32[]{:S(2)}) %all-to-all-start) | async-done | bytes 131104 | tf_op jit(solution)/shard_map/all_to_all | solution.py:329
  175.5 0.6 slice_reduce_fusion
  (96 shorter events, 5.3 us)
Async XLA Ops:
  7.2 37.4 %copy-start.10 = (s32[4]{0:T(128)S(1)}, s32[4]{0:T(128)}, u32[]{:S(2)}) copy-start(s32[4]{0:T(128)} %constant.70.clone) | copy-start | bytes 52
  7.2 123.5 %all-gather.2.cloned.1.call-start = ((), (), s32[]{:S(2)}) async-start(), calls=%async_computation.1 | async-start | bytes 3981312 | tf_op jit(solution)/shard_map/all_gather | solution.py:286
  7.2 44.2 %copy-start.9 = (s32[8]{0:T(128)S(1)}, s32[8]{0:T(128)}, u32[]{:S(2)}) copy-start(s32[8]{0:T(128)} %constant.69.clone) | copy-start | bytes 100
  8.7 6.1 %collective-permute-start.20 = (bf16[72,768]{1,0:T(8,128)(2,1)S(1)}, bf16[72,768]{1,0:T(8,128)(2,1)S(1)}, u32[]{:S(2)}, u32[]{:S(2)}) collective-permute-start(bf16[72,768]{1,0:T(8,128)(2,1)S(1)} %slice.199), channel_id=1, source_target_pairs={{0,24},{8,0},{16,8},{24,16},{1,25},{9,1},{17,9},{25,17},{2,26},{10... | collective-permute-start | bytes 331784 | tf_op jit(solution)/shard_map/ppermute | solution.py:30
  12.1 5.2 %collective-permute-start.21 = (bf16[72,768]{1,0:T(8,128)(2,1)S(1)}, bf16[72,768]{1,0:T(8,128)(2,1)S(1)}, u32[]{:S(2)}, u32[]{:S(2)}) collective-permute-start(bf16[72,768]{1,0:T(8,128)(2,1)S(1)} %slice.199), channel_id=1, source_target_pairs={{0,16},{8,24},{16,0},{24,8},{1,17},{9,25},{17,1},{25,9},{2,18},{10... | collective-permute-start | bytes 331784 | tf_op jit(solution)/shard_map/ppermute | solution.py:30
  12.6 7.9 %collective-permute-start.22 = (bf16[72,768]{1,0:T(8,128)(2,1)S(1)}, bf16[72,768]{1,0:T(8,128)(2,1)S(1)}, u32[]{:S(2)}, u32[]{:S(2)}) collective-permute-start(bf16[72,768]{1,0:T(8,128)(2,1)S(1)} %slice.199), channel_id=1, source_target_pairs={{0,8},{8,16},{16,24},{24,0},{1,9},{9,17},{17,25},{25,1},{2,10},{10... | collective-permute-start | bytes 331784 | tf_op jit(solution)/shard_map/ppermute | solution.py:30
  28.6 3.3 %collective-permute-start.15 = (f32[4,8,448]{2,1,0:T(8,128)}, f32[4,8,448]{2,1,0:T(8,128)S(1)}, u32[]{:S(2)}, u32[]{:S(2)}) collective-permute-start(f32[4,8,448]{2,1,0:T(8,128)} %get-tuple-element.13), channel_id=1, source_target_pairs={{0,24},{8,0},{16,8},{24,16},{1,25},{9,1},{17,9},{25,17},{2,26},{10... | collective-permute-start | bytes 172040 | tf_op jit(solution)/shard_map/ppermute | solution.py:30
  34.0 5.9 %collective-permute-start.16 = (f32[4,8,448]{2,1,0:T(8,128)S(1)}, f32[4,8,448]{2,1,0:T(8,128)S(1)}, u32[]{:S(2)}, u32[]{:S(2)}) collective-permute-start(f32[4,8,448]{2,1,0:T(8,128)S(1)} %select_select_fusion.4), channel_id=1, source_target_pairs={{0,16},{8,24},{16,0},{24,8},{1,17},{9,25},{17,1},{25,9},{2,18},{10... | collective-permute-start | bytes 172040 | tf_op jit(solution)/shard_map/ppermute | solution.py:30
  34.2 33.1 %collective-permute-start = (bf16[72,1024]{1,0:T(8,128)(2,1)S(1)}, bf16[72,1024]{1,0:T(8,128)(2,1)S(1)}, u32[]{:S(2)}, u32[]{:S(2)}) collective-permute-start(bf16[72,1024]{1,0:T(8,128)(2,1)S(1)} %slice.164), channel_id=1, source_target_pairs={{0,224},{32,0},{64,32},{96,64},{128,96},{160,128},{192,160},{224,1... | collective-permute-start | bytes 442376 | tf_op jit(solution)/shard_map/ppermute | solution.py:30
  39.9 27.5 %collective-permute-start.2 = (bf16[72,1024]{1,0:T(8,128)(2,1)S(1)}, bf16[72,1024]{1,0:T(8,128)(2,1)S(1)}, u32[]{:S(2)}, u32[]{:S(2)}) collective-permute-start(bf16[72,1024]{1,0:T(8,128)(2,1)S(1)} %slice.164), channel_id=1, source_target_pairs={{0,32},{32,64},{64,96},{96,128},{128,160},{160,192},{192,224},{224... | collective-permute-start | bytes 442376 | tf_op jit(solution)/shard_map/ppermute | solution.py:30
  40.1 7.7 %collective-permute-start.17 = (f32[4,8,448]{2,1,0:T(8,128)S(1)}, f32[4,8,448]{2,1,0:T(8,128)S(1)}, u32[]{:S(2)}, u32[]{:S(2)}) collective-permute-start(f32[4,8,448]{2,1,0:T(8,128)S(1)} %select_select_fusion.3), channel_id=1, source_target_pairs={{0,224},{32,0},{64,32},{96,64},{128,96},{160,128},{192,160},{224,1... | collective-permute-start | bytes 172040 | tf_op jit(solution)/shard_map/ppermute | solution.py:30
  48.0 18.1 %collective-permute-start.18 = (f32[4,8,448]{2,1,0:T(8,128)S(1)}, f32[4,8,448]{2,1,0:T(8,128)S(1)}, u32[]{:S(2)}, u32[]{:S(2)}) collective-permute-start(f32[4,8,448]{2,1,0:T(8,128)S(1)} %select_select_fusion.2), channel_id=1, source_target_pairs={{0,192},{32,224},{64,0},{96,32},{128,64},{160,96},{192,128},{224,1... | collective-permute-start | bytes 172040 | tf_op jit(solution)/shard_map/ppermute | solution.py:30
  66.3 8.7 %collective-permute-start.19 = (f32[4,8,448]{2,1,0:T(8,128)S(1)}, f32[4,8,448]{2,1,0:T(8,128)S(1)}, u32[]{:S(2)}, u32[]{:S(2)}) collective-permute-start(f32[4,8,448]{2,1,0:T(8,128)S(1)} %select_select_fusion.1), channel_id=1, source_target_pairs={{0,128},{32,160},{64,192},{96,224},{128,0},{160,32},{192,64},{224,... | collective-permute-start | bytes 172040 | tf_op jit(solution)/shard_map/ppermute | solution.py:30
  67.4 45.3 %copy-start = (bf16[216,1024]{1,0:T(8,128)(2,1)}, bf16[216,1024]{1,0:T(8,128)(2,1)S(1)}, u32[]{:S(2)}) copy-start(bf16[216,1024]{1,0:T(8,128)(2,1)S(1)} %pad_maximum_fusion.refs_0_) | copy-start | bytes 1327108
  67.4 26.8 %collective-permute-start.11 = (bf16[216,1024]{1,0:T(8,128)(2,1)S(1)}, bf16[216,1024]{1,0:T(8,128)(2,1)S(1)}, u32[]{:S(2)}, u32[]{:S(2)}) collective-permute-start(bf16[216,1024]{1,0:T(8,128)(2,1)S(1)} %pad_maximum_fusion.refs_0_), channel_id=1, source_target_pairs={{0,24},{8,0},{16,8},{24,16},{1,25},{9,1},{17,9},{25,17},{2,26},{10... | collective-permute-start | bytes 1327112 | tf_op jit(solution)/shard_map/ppermute | solution.py:30
  69.7 28.0 %collective-permute-start.12 = (bf16[216,1024]{1,0:T(8,128)(2,1)S(1)}, bf16[216,1024]{1,0:T(8,128)(2,1)S(1)}, u32[]{:S(2)}, u32[]{:S(2)}) collective-permute-start(bf16[216,1024]{1,0:T(8,128)(2,1)S(1)} %pad_maximum_fusion.refs_0_), channel_id=1, source_target_pairs={{0,8},{8,16},{16,24},{24,0},{1,9},{9,17},{17,25},{25,1},{2,10},{10... | collective-permute-start | bytes 1327112 | tf_op jit(solution)/shard_map/ppermute | solution.py:30
  69.7 10.7 %collective-permute-start.1 = (bf16[72,1024]{1,0:T(8,128)(2,1)S(1)}, bf16[72,1024]{1,0:T(8,128)(2,1)S(1)}, u32[]{:S(2)}, u32[]{:S(2)}) collective-permute-start(bf16[72,1024]{1,0:T(8,128)(2,1)S(1)} %collective-permute-done), channel_id=1, source_target_pairs={{0,224},{32,0},{64,32},{96,64},{128,96},{160,128},{192,160},{224,1... | collective-permute-start | bytes 442376 | tf_op jit(solution)/shard_map/ppermute | solution.py:30
  70.9 11.4 %collective-permute-start.3 = (bf16[72,1024]{1,0:T(8,128)(2,1)S(1)}, bf16[72,1024]{1,0:T(8,128)(2,1)S(1)}, u32[]{:S(2)}, u32[]{:S(2)}) collective-permute-start(bf16[72,1024]{1,0:T(8,128)(2,1)S(1)} %collective-permute-done.2), channel_id=1, source_target_pairs={{0,32},{32,64},{64,96},{96,128},{128,160},{160,192},{192,224},{224... | collective-permute-start | bytes 442376 | tf_op jit(solution)/shard_map/ppermute | solution.py:30
  80.4 4.3 %collective-permute-start.4 = (bf16[72,1024]{1,0:T(8,128)(2,1)S(1)}, bf16[72,1024]{1,0:T(8,128)(2,1)S(1)}, u32[]{:S(2)}, u32[]{:S(2)}) collective-permute-start(bf16[72,1024]{1,0:T(8,128)(2,1)S(1)} %collective-permute-done.1), channel_id=1, source_target_pairs={{0,224},{32,0},{64,32},{96,64},{128,96},{160,128},{192,160},{224,1... | collective-permute-start | bytes 442376 | tf_op jit(solution)/shard_map/ppermute | solution.py:30
  82.3 5.3 %collective-permute-start.5 = (bf16[72,1024]{1,0:T(8,128)(2,1)S(1)}, bf16[72,1024]{1,0:T(8,128)(2,1)S(1)}, u32[]{:S(2)}, u32[]{:S(2)}) collective-permute-start(bf16[72,1024]{1,0:T(8,128)(2,1)S(1)} %collective-permute-done.3), channel_id=1, source_target_pairs={{0,32},{32,64},{64,96},{96,128},{128,160},{160,192},{192,224},{224... | collective-permute-start | bytes 442376 | tf_op jit(solution)/shard_map/ppermute | solution.py:30
  84.7 4.8 %collective-permute-start.6 = (bf16[72,1024]{1,0:T(8,128)(2,1)S(1)}, bf16[72,1024]{1,0:T(8,128)(2,1)S(1)}, u32[]{:S(2)}, u32[]{:S(2)}) collective-permute-start(bf16[72,1024]{1,0:T(8,128)(2,1)S(1)} %collective-permute-done.4), channel_id=1, source_target_pairs={{0,224},{32,0},{64,32},{96,64},{128,96},{160,128},{192,160},{224,1... | collective-permute-start | bytes 442376 | tf_op jit(solution)/shard_map/ppermute | solution.py:30
  89.5 23.2 %copy-start.3 = (bf16[360,1024]{1,0:T(8,128)(2,1)}, bf16[360,1024]{1,0:T(8,128)(2,1)S(1)}, u32[]{:S(2)}) copy-start(bf16[360,1024]{1,0:T(8,128)(2,1)S(1)} %constant_dynamic-update-slice_fusion.refs_4_) | copy-start | bytes 2211844
  89.6 31.1 %collective-permute-start.7 = (bf16[360,1024]{1,0:T(8,128)(2,1)S(1)}, bf16[360,1024]{1,0:T(8,128)(2,1)S(1)}, u32[]{:S(2)}, u32[]{:S(2)}) collective-permute-start(bf16[360,1024]{1,0:T(8,128)(2,1)S(1)} %constant_dynamic-update-slice_fusion.refs_4_), channel_id=1, source_target_pairs={{0,24},{8,0},{16,8},{24,16},{1,25},{9,1},{17,9},{25,17},{2,26},{10... | collective-permute-start | bytes 2211848 | tf_op jit(solution)/shard_map/ppermute | solution.py:30
  92.0 28.5 %collective-permute-start.9 = (bf16[360,1024]{1,0:T(8,128)(2,1)S(1)}, bf16[360,1024]{1,0:T(8,128)(2,1)S(1)}, u32[]{:S(2)}, u32[]{:S(2)}) collective-permute-start(bf16[360,1024]{1,0:T(8,128)(2,1)S(1)} %constant_dynamic-update-slice_fusion.refs_4_), channel_id=1, source_target_pairs={{0,8},{8,16},{16,24},{24,0},{1,9},{9,17},{17,25},{25,1},{2,10},{10... | collective-permute-start | bytes 2211848 | tf_op jit(solution)/shard_map/ppermute | solution.py:30
  92.1 0.6 copy-start.8
  94.1 18.6 %copy-start.4 = (bf16[216,1024]{1,0:T(8,128)(2,1)}, bf16[216,1024]{1,0:T(8,128)(2,1)S(1)}, u32[]{:S(2)}) copy-start(bf16[216,1024]{1,0:T(8,128)(2,1)S(1)} %collective-permute-done.11.refs_1_) | copy-start | bytes 1327108
  94.9 12.9 %collective-permute-start.13 = (bf16[216,512]{1,0:T(8,128)(2,1)}, bf16[216,512]{1,0:T(8,128)(2,1)}, u32[]{:S(2)}, u32[]{:S(2)}) collective-permute-start(bf16[216,512]{1,0:T(8,128)(2,1)} %slice.167), channel_id=1, source_target_pairs={{0,24},{8,0},{16,8},{24,16},{1,25},{9,1},{17,9},{25,17},{2,26},{10... | collective-permute-start | bytes 663560 | tf_op jit(solution)/shard_map/ppermute | solution.py:30
  97.6 15.1 %copy-start.5 = (bf16[216,1024]{1,0:T(8,128)(2,1)}, bf16[216,1024]{1,0:T(8,128)(2,1)S(1)}, u32[]{:S(2)}) copy-start(bf16[216,1024]{1,0:T(8,128)(2,1)S(1)} %collective-permute-done.12.refs_2_) | copy-start | bytes 1327108
  98.4 12.5 %collective-permute-start.14 = (bf16[216,512]{1,0:T(8,128)(2,1)}, bf16[216,512]{1,0:T(8,128)(2,1)}, u32[]{:S(2)}, u32[]{:S(2)}) collective-permute-start(bf16[216,512]{1,0:T(8,128)(2,1)} %slice.168), channel_id=1, source_target_pairs={{0,8},{8,16},{16,24},{24,0},{1,9},{9,17},{17,25},{25,1},{2,10},{10... | collective-permute-start | bytes 663560 | tf_op jit(solution)/shard_map/ppermute | solution.py:30
  120.5 2.9 %copy-start.2 = (bf16[360,1024]{1,0:T(8,128)(2,1)}, bf16[360,1024]{1,0:T(8,128)(2,1)S(1)}, u32[]{:S(2)}) copy-start(bf16[360,1024]{1,0:T(8,128)(2,1)S(1)} %collective-permute-done.9.refs_1_) | copy-start | bytes 2211844
  120.5 18.6 %collective-permute-start.10 = (bf16[360,512]{1,0:T(8,128)(2,1)S(1)}, bf16[360,512]{1,0:T(8,128)(2,1)S(1)}, u32[]{:S(2)}, u32[]{:S(2)}) collective-permute-start(bf16[360,512]{1,0:T(8,128)(2,1)S(1)} %slice.166), channel_id=1, source_target_pairs={{0,8},{8,16},{16,24},{24,0},{1,9},{9,17},{17,25},{25,1},{2,10},{10... | collective-permute-start | bytes 1105928 | tf_op jit(solution)/shard_map/ppermute | solution.py:30
  120.6 2.8 %copy-start.1 = (bf16[360,1024]{1,0:T(8,128)(2,1)}, bf16[360,1024]{1,0:T(8,128)(2,1)S(1)}, u32[]{:S(2)}) copy-start(bf16[360,1024]{1,0:T(8,128)(2,1)S(1)} %collective-permute-done.7.refs_0_) | copy-start | bytes 2211844
  120.7 18.5 %collective-permute-start.8 = (bf16[360,512]{1,0:T(8,128)(2,1)S(1)}, bf16[360,512]{1,0:T(8,128)(2,1)S(1)}, u32[]{:S(2)}, u32[]{:S(2)}) collective-permute-start(bf16[360,512]{1,0:T(8,128)(2,1)S(1)} %slice.165), channel_id=1, source_target_pairs={{0,24},{8,0},{16,8},{24,16},{1,25},{9,1},{17,9},{25,17},{2,26},{10... | collective-permute-start | bytes 1105928 | tf_op jit(solution)/shard_map/ppermute | solution.py:30
  139.1 0.7 copy-start.6
  139.2 0.9 copy-start.7
  146.4 29.1 %all-to-all-start = ((f32[256,1,128]{2,1,0:T(1,128)}), f32[256,1,128]{2,1,0:T(1,128)S(1)}, u32[]{:S(2)}, u32[]{:S(2)}) async-start(f32[256,1,128]{2,1,0:T(1,128)} %bitcast.88), calls=%async_computation | async-start | bytes 262144 | tf_op jit(solution)/shard_map/all_to_all | solution.py:329
Sparse Core Ops, SparseCore 0:
  21.6 60.3 all-gather.1

commit v2 on v0

v2 whole, which is shorter than its diff:
```python
import jax
import jax.numpy as jnp
from jax import lax
from jax.experimental import pallas as pl
from jax.experimental.pallas import tpu as pltpu
from jax.sharding import Mesh
from jax.sharding import PartitionSpec as P

D = 3584
LAYERS = 4
SEQ = ("seq_0", "seq_1")
FEAT = ("feat_0", "feat_1")
ALL = SEQ + FEAT
NZ, NX = 8, 4
epsilon = 1e-05

C_COLS = 768
HALF = 512
BN = 256
VMEM = 20 * 1024 * 1024
C_FIRST = True
SC_AFTER = (2, -2, 3, -3)

Z_ORDER = (0, 1, -1, 2, -2, 3, -3, 4)
X_ORDER = (0, 1, -1, 2)
f32 = jnp.float32
bf16 = jnp.bfloat16


def shift(value, axis, size, by):
    return lax.ppermute(value, axis, [(i, (i - by) % size) for i in range(size)])


def from_z(value, by):
    return shift(value, "seq_0", NZ, by)


def from_x(value, by):
    return shift(value, "seq_1", NX, by)


def params(**kw):
    return pltpu.CompilerParams(vmem_limit_bytes=VMEM, **kw)


def stay(value):
    return pltpu.with_memory_space_constraint(value, pltpu.HBM)


def moments_kernel(pick, teacher, weight, chosen, stats):
    x16 = teacher[0]
    chosen[0] = x16
    x = x16.astype(f32)
    w = weight[...]
    count = jnp.sum(w, axis=1, keepdims=True)
    mean = jnp.sum(x * w, axis=1, keepdims=True) / jnp.maximum(count, 1.0)
    centred = x - mean
    spread = jnp.sum(w * centred * centred, axis=1, keepdims=True)
    lane = lax.broadcasted_iota(jnp.int32, (x.shape[0], 128), 1)
    table = jnp.where(lane == 0, mean, jnp.where(lane == 1, spread, count))
    stats[0] = table.T[:8]


def local_moments(teacher, weight, pick):
    layers, features, tokens = teacher.shape
    return pl.pallas_call(
        moments_kernel,
        grid_spec=pltpu.PrefetchScalarGridSpec(
            num_scalar_prefetch=1,
            grid=(layers,),
            in_specs=[
                pl.BlockSpec((1, features, tokens), lambda i, p: (p[i], 0, 0)),
                pl.BlockSpec((1, tokens), lambda i, p: (0, 0)),
            ],
            out_specs=[
                pl.BlockSpec((1, features, tokens), lambda i, p: (i, 0, 0)),
                pl.BlockSpec((1, 8, features), lambda i, p: (i, 0, 0)),
            ],
        ),
        out_shape=[
            jax.ShapeDtypeStruct((layers, features, tokens), bf16),
            jax.ShapeDtypeStruct((layers, 8, features), f32),
        ],
        compiler_params=params(),
        cost_estimate=pl.CostEstimate(flops=20_000_000, bytes_accessed=8_000_000, transcendentals=0),
        name="moments",
    )(pick, stay(teacher), weight)


def merged(groups):
    mean, spread, count = ([g[:, k] for g in groups] for k in range(3))
    joined = sum(count)
    whole = jnp.maximum(joined, 1.0)
    middle = mean[0] + sum(n * (m - mean[0]) for m, n in zip(mean[1:], count[1:])) / whole
    around = sum(spread) + sum(n * (m - middle) * (m - middle) for m, n in zip(mean, count))
    row = lax.broadcasted_iota(jnp.int32, groups[0].shape, 1)
    return jnp.where(row == 0, middle[:, None], jnp.where(row == 1, around[:, None], joined[:, None]))


def place_kernel(zs, *refs):
    *pieces, out = refs
    for k, piece in enumerate(pieces):
        out[zs[k]] = piece[...]


def placed(pieces, zs):
    rows, cols = pieces[0].shape
    n = len(pieces)
    return pl.pallas_call(
        place_kernel,
        in_specs=[pl.BlockSpec(memory_space=pltpu.SMEM)] + [pl.BlockSpec(memory_space=pltpu.VMEM)] * n,
        out_specs=pl.BlockSpec(memory_space=pltpu.VMEM),
        out_shape=jax.ShapeDtypeStruct((n, rows, cols), bf16),
        compiler_params=params(),
        cost_estimate=pl.CostEstimate(flops=0, bytes_accessed=2_500_000, transcendentals=0),
        name="placed",
    )(zs, *pieces).reshape(n * rows, cols)


def columns_kernel(rows, student, out):
    order = [i * NX + j for j in range(NX) for i in range(NZ)]
    out[...] = jnp.concatenate([student[:, pl.ds(k * rows, rows)] for k in order], axis=1)


def by_x(student, rows):
    tokens, depth = student.shape
    block = 256
    return pl.pallas_call(
        lambda *refs: columns_kernel(rows, *refs),
        grid=(tokens // block,),
        in_specs=[pl.BlockSpec((block, depth), lambda i: (i, 0))],
        out_specs=pl.BlockSpec((block, depth), lambda i: (i, 0)),
        out_shape=jax.ShapeDtypeStruct((tokens, depth), bf16),
        compiler_params=params(),
        cost_estimate=pl.CostEstimate(flops=0, bytes_accessed=10_000_000, transcendentals=0),
        name="columns_by_x",
    )(student)


def dot(weights, student):
    return lax.dot_general(weights, student, (((0,), (1,)), ((), ())), preferred_element_type=f32)


def product_kernel(steps, parts, lefts, first, xs, student, *refs):
    if parts == 1:
        weights = refs[0][...]
        refs = refs[1:]
    else:
        *refs, joined = refs
        for k in range(parts - 1):
            joined[xs[k]] = refs[k][...]
        left = pl.program_id(0) < lefts
        joined[xs[parts - 1]] = jnp.where(left, refs[parts - 1][...], refs[parts][...])
        weights = joined[...].reshape(student.shape[1], BN)
        refs = refs[parts + 1 :]
    predicted = dot(weights, student[...])
    chosen, scale, weight = refs[:3]
    if first:
        error, loss, sums = refs[3:]
    else:
        loss_in, _, error, loss, sums = refs[3:]
    i = pl.program_id(0)

    @pl.when(i == 0)
    def _():
        sums[...] = jnp.zeros_like(sums) if first else loss_in[...]

    target = (chosen[...].astype(f32) - scale[:, 0:1]) * scale[:, 1:2]
    residual = predicted - target
    masked = weight[...] * residual
    error[...] = masked.astype(bf16)
    sums[...] += jnp.sum(masked * residual, axis=0, keepdims=True)

    @pl.when(i == steps - 1)
    def _():
        if first:
            loss[...] = sums[...]
        else:
            loss[...] = jnp.broadcast_to(jnp.sum(sums[...], axis=1, keepdims=True), loss.shape)


def product(student, weights, xs, chosen, scale, weight, start, before=None, copies=None):
    tokens, depth = student.shape
    parts = max(len(weights) - 1, 1)
    k = depth // parts
    cols = weights[0].shape[1]
    steps, at = cols // BN, start // BN
    first = before is None
    lefts = weights[-2].shape[1] // BN if parts > 1 else 0
    in_specs = [pl.BlockSpec(memory_space=pltpu.VMEM)]
    whole = len(weights) - 2 if parts > 1 else 1
    in_specs += [pl.BlockSpec((k, BN), lambda i, p: (0, i))] * whole
    if parts > 1:
        in_specs += [
            pl.BlockSpec((k, BN), lambda i, p: (0, jnp.minimum(i, lefts - 1))),
            pl.BlockSpec((k, BN), lambda i, p: (0, jnp.maximum(i - lefts, 0))),
        ]
    in_specs += [
        pl.BlockSpec((BN, tokens), lambda i, p: (i + at, 0)),
        pl.BlockSpec((BN, 2), lambda i, p: (i + at, 0)),
        pl.BlockSpec((1, tokens), lambda i, p: (0, 0)),
    ]
    args = [xs, student, *weights, stay(chosen), scale, weight]
    if not first:
        in_specs += [pl.BlockSpec((1, tokens), lambda i, p: (0, 0)), pl.BlockSpec(memory_space=pl.ANY)]
        args += list(before)
    loss = (1, tokens) if first else (copies, 128)
    return pl.pallas_call(
        lambda *refs: product_kernel(steps, parts, lefts, first, *refs),
        grid_spec=pltpu.PrefetchScalarGridSpec(
            num_scalar_prefetch=1,
            grid=(steps,),
            in_specs=in_specs,
            out_specs=[
                pl.BlockSpec((BN, tokens), lambda i, p: (i + at, 0)),
                pl.BlockSpec(loss, lambda i, p: (0, 0)),
            ],
            scratch_shapes=[pltpu.VMEM((1, tokens), f32)] + ([pltpu.VMEM((parts, k, BN), bf16)] if parts > 1 else []),
        ),
        out_shape=[
            jax.ShapeDtypeStruct(chosen.shape, bf16),
            jax.ShapeDtypeStruct(loss, f32),
        ],
        input_output_aliases={} if first else {len(args) - 1: 0},
        compiler_params=params(),
        cost_estimate=pl.CostEstimate(flops=2 * depth * cols * tokens, bytes_accessed=14_000_000, transcendentals=0),
        name="product",
    )(*args)


def after(value, *done):
    return lax.optimization_barrier((value, *done))[0]


def shards(teacher_states, student_states, projection, layer_pick, validity):
    z, x = lax.axis_index("seq_0"), lax.axis_index("seq_1")
    layers, rows, features = projection.shape
    tokens = student_states.shape[0]
    columns = layers * features

    mine = jnp.transpose(projection, (1, 0, 2)).reshape(rows, columns)
    c_mine, b_mine = mine[:, :C_COLS], mine[:, C_COLS:]

    c_next, c_last, c_far = from_x(c_mine, 1), from_x(c_mine, -1), from_x(c_mine, 2)
    line = {0: b_mine, 1: from_z(b_mine, 1), -1: from_z(b_mine, -1), 2: from_z(b_mine, 2), -2: from_z(b_mine, -2)}
    place = lax.broadcasted_iota(jnp.int32, (NX, 1, 1), 0)
    away = (place - x) % NX
    c_block = jnp.where(
        away == 0, c_mine[None], jnp.where(away == 1, c_next[None], jnp.where(away == 2, c_far[None], c_last[None]))
    ).reshape(NX * rows, C_COLS)
    line[3], line[-3], line[4] = from_z(line[2], 1), from_z(line[-2], -1), from_z(line[2], 2)

    weight = validity.astype(f32).reshape(1, tokens)
    chosen, stats = local_moments(
        jnp.transpose(teacher_states, (0, 2, 1)), after(weight, line[3], line[-3]), layer_pick
    )
    c_weights = lax.all_gather(after(c_block, *[line[k] for k in SC_AFTER]), "seq_0", axis=0, tiled=True)

    zs = (z + jnp.asarray(Z_ORDER, jnp.int32)) % NZ
    xs = (x + jnp.asarray(X_ORDER, jnp.int32)) % NX
    *line, zs, xs, stats = lax.optimization_barrier((*[line[k] for k in Z_ORDER], zs, xs, stats))

    own = placed(line, zs)
    x_after, x_before = from_x(own, 1), from_x(own, -1)
    student = by_x(after(student_states, own), rows)
    stats = merged([stats] + [from_x(stats, by) for by in (1, -1, 2)])
    stats = merged([stats] + [from_z(stats, by) for by in Z_ORDER[1:]])
    counted = stats[0, 2, 0]
    scale = jnp.stack(
        [stats[:, 0].reshape(columns), (1.0 / jnp.sqrt(stats[:, 1] / stats[:, 2] + epsilon)).reshape(columns)], axis=1
    )
    x_left, x_right = from_x(x_after[:, :HALF], 1), from_x(x_before[:, HALF:], -1)

    chosen = chosen.reshape(columns, tokens)
    copies = NZ * NX * lax.axis_size("feat_0") * lax.axis_size("feat_1")
    b_args = (student, [own, x_after, x_before, x_left, x_right], xs, chosen, scale, weight, C_COLS)
    c_args = (student_states, [stay(c_weights)], xs, chosen, scale, weight, 0)
    if C_FIRST:
        error, loss = product(*c_args)
        error, loss = product(*b_args, (loss, error), copies)
    else:
        error, loss = product(*b_args)
        error, loss = product(*c_args, (loss, error), copies)
    squares = jnp.sum(lax.all_to_all(loss, ALL, 0, 0, tiled=True)[:, 0])
    total_loss = squares / (counted * D * LAYERS)
    whitened = jnp.transpose(error.reshape(layers, features, tokens), (0, 2, 1))
    return whitened, total_loss


def solution(mesh):
    torus = Mesh(mesh.devices.reshape(NZ, NX, 4, 2), ALL)
    in_specs = (P(None, SEQ, FEAT), P(SEQ, None), P(None, SEQ, FEAT), P(), P(SEQ))
    out_specs = (P(None, SEQ, FEAT), P())
    return jax.shard_map(shards, mesh=torus, in_specs=in_specs, out_specs=out_specs, check_vma=False)
```

time: 186 us -> 145 us (0.78)
  blocking collectives: 74.1 us -> 0 us
  starting transfers between devices: 0.04 us -> 53.6 us
  Pallas kernels: 0 us -> 27.9 us
  matrix products: 19.1 us -> 0 us
  waiting for transfers between devices: 46.9 us -> 29.2 us
  between operations: 30.6 us -> 16.7 us
  local copies, waits for them, and re-layouts: 6.71 us -> 12.4 us
  other arithmetic: 8.52 us -> 4.59 us
    ppermute x0 -> x24, starting transfers between devices: none -> 43.2 us  [shift(): lax.ppermute(value, axis, [(i, (i - by) % size) for i in range(size)])]
    psum x4 -> x0, blocking collectives: 40 us -> none  [over_axes(): return functools.reduce(lax.psum, axes, value)]
    all_gather x1, waiting for transfers between devices: 46.2 us -> 8.06 us  [shards(): lax.all_gather(after(c_block, *[line[k] for k in SC_AFTER]), 'seq_0', axi...]
    all_gather x2 -> x0, blocking collectives: 34 us -> none  [all_in_one(): both, at, found = (lax.all_gather(jnp.concatenate(lines), axis), 0, {})]
    pallas_call x0 -> x5, Pallas kernels: none -> 27.9 us  [the longest x2 19 us: product(): pl.pallas_call(lambda *refs: product_kernel(steps, parts, lefts, first, *...]
    dot_general x1 -> x0, matrix products: 19.1 us -> none  [shards(): jnp.einsum('tr,lrd->ltd', student_states, all_weights, preferred_element_...]
    all_to_all x0 -> x1, waiting for transfers between devices: none -> 11.8 us  [shards(): squares = jnp.sum(lax.all_to_all(loss, ALL, 0, 0, tiled=True)[:, 0])]
    all_to_all x0 -> x1, starting transfers between devices: none -> 10.5 us  [shards(): squares = jnp.sum(lax.all_to_all(loss, ALL, 0, 0, tiled=True)[:, 0])]
  transfers between devices with their start and end apart: 1 -> 26, of which waited for: 1 -> 7; matrix products, arithmetic and copies ran while one was open for 8% -> 5% of each run, Pallas kernels for 0% -> 12%
where the time goes in v2:
time: 145 us; the launch traced here: 144 us
  starting transfers between devices  53.6 us (37%)
  waiting for transfers between devices  29.2 us (20%)
  Pallas kernels  27.9 us (19%)
  between operations  16.7 us (12%)
  local copies, waits for them, and re-layouts  12.4 us (9%)
  other arithmetic  4.59 us (3%)
    ppermute x24, starting transfers between devices, shift(): lax.ppermute(value, axis, [(i, (i - by) % size) for i in range(size)])  43.2 us
    pallas_call x2, Pallas kernels, product(): pl.pallas_call(lambda *refs: product_kernel(steps, parts, lefts, first, *...  19 us
    all_to_all x1, waiting for transfers between devices, shards(): squares = jnp.sum(lax.all_to_all(loss, ALL, 0, 0, tiled=True)[:, 0])  11.8 us
    all_to_all x1, starting transfers between devices, shards(): squares = jnp.sum(lax.all_to_all(loss, ALL, 0, 0, tiled=True)[:, 0])  10.5 us
    ppermute x24, waiting for transfers between devices, shift(): lax.ppermute(value, axis, [(i, (i - by) % size) for i in range(size)])  9.29 us
    all_gather x1, waiting for transfers between devices, shards(): lax.all_gather(after(c_block, *[line[k] for k in SC_AFTER]), 'seq_0', axi...  8.06 us
    unnamed x27, local copies, waits for them, and re-layouts  7.69 us
    pallas_call x1, Pallas kernels, local_moments(): pl.pallas_call(moments_kernel, grid_spec=pltpu.PrefetchScalarGridSpec(num...  4.81 us
  transfers between devices with their start and end apart: 26, of which 7 were waited for; matrix products, arithmetic and copies ran while one was open for 5% of the time, Pallas kernels for 12%

profile of v2, /device:TPU:1, one launch (start us, length us, event | category | flops | bytes accessed | tf_op | source)
XLA Modules:
  0.0 144.4 jit_solution(9863290059801666626)
XLA Ops:
  7.2 1.1 copy.18
  8.6 3.9 %collective-permute-start.3 = (bf16[72,1024]{1,0:T(8,128)(2,1)S(1)}, bf16[72,1024]{1,0:T(8,128)(2,1)S(1)}, u32[]{:S(2)}, u32[]{:S(2)}) collective-permute-start(bf16[72,1024]{1,0:T(8,128)(2,1)S(1)} %slice.180.refs_0_), channel_id=1, source_target_pairs={{0,64},{32,96},{64,128},{96,160},{128,192},{160,224},{192,0},{224,... | collective-permute-start | bytes 442376 | tf_op jit(solution)/shard_map/ppermute | solution.py:31
  12.5 3.1 %collective-permute-start.2 = (bf16[72,1024]{1,0:T(8,128)(2,1)S(1)}, bf16[72,1024]{1,0:T(8,128)(2,1)S(1)}, u32[]{:S(2)}, u32[]{:S(2)}) collective-permute-start(bf16[72,1024]{1,0:T(8,128)(2,1)S(1)} %slice.180.refs_0_), channel_id=1, source_target_pairs={{0,192},{32,224},{64,0},{96,32},{128,64},{160,96},{192,128},{224,1... | collective-permute-start | bytes 442376 | tf_op jit(solution)/shard_map/ppermute | solution.py:31
  15.7 1.3 collective-permute-start.23
  17.0 2.5 %collective-permute-start.22 = (bf16[72,768]{1,0:T(8,128)(2,1)S(1)}, bf16[72,768]{1,0:T(8,128)(2,1)S(1)}, u32[]{:S(2)}, u32[]{:S(2)}) collective-permute-start(bf16[72,768]{1,0:T(8,128)(2,1)S(1)} %slice.219), channel_id=1, source_target_pairs={{0,16},{8,24},{16,0},{24,8},{1,17},{9,25},{17,1},{25,9},{2,18},{10... | collective-permute-start | bytes 331784 | tf_op jit(solution)/shard_map/ppermute | solution.py:31
  19.4 1.2 collective-permute-start.21
  20.6 2.8 %collective-permute-start.5 = (bf16[72,1024]{1,0:T(8,128)(2,1)S(1)}, bf16[72,1024]{1,0:T(8,128)(2,1)S(1)}, u32[]{:S(2)}, u32[]{:S(2)}) collective-permute-start(bf16[72,1024]{1,0:T(8,128)(2,1)S(1)} %collective-permute-done.3.refs_4_), channel_id=1, source_target_pairs={{0,32},{32,64},{64,96},{96,128},{128,160},{160,192},{192,224},{224... | collective-permute-start | bytes 442376 | tf_op jit(solution)/shard_map/ppermute | solution.py:31
  23.3 0.4 collective-permute-done.2.refs_3_
  23.7 0.5 collective-permute-start.4
  24.7 1.0 fusion.1
  25.7 1.5 %collective-permute-done.5.refs_6_ = bf16[72,1024]{1,0:T(8,128)(2,1)S(1)} collective-permute-done((bf16[72,1024]{1,0:T(8,128)(2,1)S(1)}, bf16[72,1024]{1,0:T(8,128)(2,1)S(1)}, u32[]{:S(2)}, u32[]{:S(2)}) %collective-permute-start.5) | collective-permute-done | bytes 147488 | tf_op jit(solution)/shard_map/ppermute | solution.py:31
  27.2 0.9 collective-permute-done.4.refs_5_
  28.1 2.0 %collective-permute-start.1 = (bf16[72,1024]{1,0:T(8,128)(2,1)S(1)}, bf16[72,1024]{1,0:T(8,128)(2,1)S(1)}, u32[]{:S(2)}, u32[]{:S(2)}) collective-permute-start(bf16[72,1024]{1,0:T(8,128)(2,1)S(1)} %slice.180.refs_0_), channel_id=1, source_target_pairs={{0,32},{32,64},{64,96},{96,128},{128,160},{160,192},{192,224},{224... | collective-permute-start | bytes 442376 | tf_op jit(solution)/shard_map/ppermute | solution.py:31
  30.1 0.8 collective-permute-start
  30.9 0.8 convert_element_type.3
  31.7 0.8 and_select_fusion.1.refs_0_
  32.6 1.0 collective-permute-start.6
  33.6 0.7 and_select_fusion.2.zs
  34.3 0.7 copy-done.7
  35.0 4.8 %moments.1 = (bf16[4,448,1024]{2,1,0:T(8,128)(2,1)S(1)}, f32[4,8,448]{2,1,0:T(8,128)S(1)}) custom-call(s32[4]{0:T(128)S(1)} %copy-done.7, bf16[4,448,1024]{2,1,0:T(8,128)(2,1)} %bitcast.51, f32[1,1024]{1,0:T(1,128)S(1)} %bitcast.46), custom_call_target="tpu_custom_call" | custom-call | flops 20000000 | bytes 8000000 | tf_op jit(solution)/shard_map/moments/pallas_call | solution.py:66
  39.8 1.9 %copy-done.8 = bf16[4,448,1024]{2,1,0:T(8,128)(2,1)} copy-done((bf16[4,448,1024]{2,1,0:T(8,128)(2,1)}, bf16[4,448,1024]{2,1,0:T(8,128)(2,1)S(1)}, u32[]{:S(2)}) %copy-start.8) | copy-done | bytes 3670040
  41.7 2.8 %collective-permute-start.13 = (f32[4,8,448]{2,1,0:T(8,128)S(1)}, f32[4,8,448]{2,1,0:T(8,128)S(1)}, u32[]{:S(2)}, u32[]{:S(2)}) collective-permute-start(f32[4,8,448]{2,1,0:T(8,128)S(1)} %get-tuple-element.36), channel_id=1, source_target_pairs={{0,16},{8,24},{16,0},{24,8},{1,17},{9,25},{17,1},{25,9},{2,18},{10... | collective-permute-start | bytes 172040 | tf_op jit(solution)/shard_map/ppermute | solution.py:31
  44.8 2.4 %collective-permute-start.11 = (f32[4,8,448]{2,1,0:T(8,128)S(1)}, f32[4,8,448]{2,1,0:T(8,128)S(1)}, u32[]{:S(2)}, u32[]{:S(2)}) collective-permute-start(f32[4,8,448]{2,1,0:T(8,128)S(1)} %get-tuple-element.36), channel_id=1, source_target_pairs={{0,24},{8,0},{16,8},{24,16},{1,25},{9,1},{17,9},{25,17},{2,26},{10... | collective-permute-start | bytes 172040 | tf_op jit(solution)/shard_map/ppermute | solution.py:31
  47.2 0.6 placed.1
  47.9 2.7 %collective-permute-start.7 = (bf16[576,1024]{1,0:T(8,128)(2,1)S(1)}, bf16[576,1024]{1,0:T(8,128)(2,1)S(1)}, u32[]{:S(2)}, u32[]{:S(2)}) collective-permute-start(bf16[576,1024]{1,0:T(8,128)(2,1)S(1)} %bitcast.44), channel_id=1, source_target_pairs={{0,24},{8,0},{16,8},{24,16},{1,25},{9,1},{17,9},{25,17},{2,26},{10... | collective-permute-start | bytes 3538952 | tf_op jit(solution)/shard_map/ppermute | solution.py:31
  50.8 4.2 %collective-permute-start.20 = (f32[4,8,448]{2,1,0:T(8,128)S(1)}, f32[4,8,448]{2,1,0:T(8,128)S(1)}, u32[]{:S(2)}, u32[]{:S(2)}) collective-permute-start(f32[4,8,448]{2,1,0:T(8,128)S(1)} %select_select_fusion.1), channel_id=1, source_target_pairs={{0,128},{32,160},{64,192},{96,224},{128,0},{160,32},{192,64},{224,... | collective-permute-start | bytes 172040 | tf_op jit(solution)/shard_map/ppermute | solution.py:31
  55.2 4.3 %collective-permute-start.18 = (f32[4,8,448]{2,1,0:T(8,128)S(1)}, f32[4,8,448]{2,1,0:T(8,128)S(1)}, u32[]{:S(2)}, u32[]{:S(2)}) collective-permute-start(f32[4,8,448]{2,1,0:T(8,128)S(1)} %select_select_fusion.1), channel_id=1, source_target_pairs={{0,160},{32,192},{64,224},{96,0},{128,32},{160,64},{192,96},{224,1... | collective-permute-start | bytes 172040 | tf_op jit(solution)/shard_map/ppermute | solution.py:31
  59.5 2.6 %collective-permute-start.17 = (f32[4,8,448]{2,1,0:T(8,128)S(1)}, f32[4,8,448]{2,1,0:T(8,128)S(1)}, u32[]{:S(2)}, u32[]{:S(2)}) collective-permute-start(f32[4,8,448]{2,1,0:T(8,128)S(1)} %select_select_fusion.1), channel_id=1, source_target_pairs={{0,64},{32,96},{64,128},{96,160},{128,192},{160,224},{192,0},{224,... | collective-permute-start | bytes 172040 | tf_op jit(solution)/shard_map/ppermute | solution.py:31
  62.1 2.9 %collective-permute-done.19 = f32[4,8,448]{2,1,0:T(8,128)S(1)} collective-permute-done((f32[4,8,448]{2,1,0:T(8,128)S(1)}, f32[4,8,448]{2,1,0:T(8,128)S(1)}, u32[]{:S(2)}, u32[]{:S(2)}) %collective-permute-start.19) | collective-permute-done | bytes 57376 | tf_op jit(solution)/shard_map/ppermute | solution.py:31
  65.0 1.1 collective-permute-start.16
  66.4 3.6 %collective-permute-done.17 = f32[4,8,448]{2,1,0:T(8,128)S(1)} collective-permute-done((f32[4,8,448]{2,1,0:T(8,128)S(1)}, f32[4,8,448]{2,1,0:T(8,128)S(1)}, u32[]{:S(2)}, u32[]{:S(2)}) %collective-permute-start.17) | collective-permute-done | bytes 57376 | tf_op jit(solution)/shard_map/ppermute | solution.py:31
  69.9 0.9 collective-permute-start.14
  70.8 3.4 %columns_by_x.1.refs_1_ = bf16[1024,2304]{1,0:T(8,128)(2,1)S(1)} custom-call(bf16[1024,2304]{1,0:T(8,128)(2,1)S(1)} %copy-done), custom_call_target="tpu_custom_call" | custom-call | bytes 10000000 | tf_op jit(solution)/shard_map/columns_by_x/pallas_call | solution.py:128
  74.3 2.1 %copy-done.2 = bf16[1024,2304]{1,0:T(8,128)(2,1)} copy-done((bf16[1024,2304]{1,0:T(8,128)(2,1)}, bf16[1024,2304]{1,0:T(8,128)(2,1)S(1)}, u32[]{:S(2)}) %copy-start.2) | copy-done | bytes 4718616
  76.8 0.9 slice.182
  77.7 0.3 copy-done.3
  78.1 0.9 slice.181
  78.9 0.3 copy-done.5
  79.3 2.4 %collective-permute-start.9 = (bf16[576,512]{1,0:T(8,128)(2,1)}, bf16[576,512]{1,0:T(8,128)(2,1)}, u32[]{:S(2)}, u32[]{:S(2)}) collective-permute-start(bf16[576,512]{1,0:T(8,128)(2,1)} %slice.181), channel_id=1, source_target_pairs={{0,24},{8,0},{16,8},{24,16},{1,25},{9,1},{17,9},{25,17},{2,26},{10... | collective-permute-start | bytes 1769480 | tf_op jit(solution)/shard_map/ppermute | solution.py:31
  81.9 0.3 copy.20.refs_4_.refs_8_
  82.2 8.1 %all-gather.2.cloned.1.call-done.refs_2_ = bf16[2304,768]{1,0:T(8,128)(2,1)} async-done(((bf16[288,768]{1,0:T(8,128)(2,1)}), bf16[2304,768]{1,0:T(8,128)(2,1)}) %all-gather.2.cloned.1.call-update) | async-done | bytes 3538960 | tf_op jit(solution)/shard_map/all_gather | solution.py:257
  90.3 2.3 %copy-done.1 = bf16[1024,2304]{1,0:T(8,128)(2,1)S(1)} copy-done((bf16[1024,2304]{1,0:T(8,128)(2,1)S(1)}, bf16[1024,2304]{1,0:T(8,128)(2,1)}, u32[]{:S(2)}) %copy-start.1) | copy-done | bytes 4718616
  92.6 8.4 %product.2 = (bf16[1792,1024]{1,0:T(8,128)(2,1)}, f32[1,1024]{1,0:T(1,128)S(1)}) custom-call(s32[4]{0:T(128)S(1)} %and_select_fusion.1.refs_0_, bf16[1024,2304]{1,0:T(8,128)(2,1)S(1)} %copy-done.1, bf16[2304,768]{1,0:T(8,128)(2,1)} %all-gather.2.cloned.1.call-done.refs_2_, bf16[1792,1024]{1,0:T(8,128)(2,1)} %bitcast.49, f32[1792,2]{1,0:T(8,128)S(1)} %copy.20.refs_4_.refs_8_, ...), custom_call_target="tpu_custom_call" | custom-call | flops 3623878656 | bytes 14000000 | tf_op jit(solution)/shard_map/product/pallas_call | solution.py:208
  101.1 10.6 %product.3 = (bf16[1792,1024]{1,0:T(8,128)(2,1)}, f32[256,128]{1,0:T(8,128)}) custom-call(s32[4]{0:T(128)S(1)} %and_select_fusion.1.refs_0_, bf16[1024,2304]{1,0:T(8,128)(2,1)S(1)} %bitcast.42, bf16[576,1024]{1,0:T(8,128)(2,1)S(1)} %bitcast.45, bf16[576,1024]{1,0:T(8,128)(2,1)S(1)} %copy-done.6, ...), custom_call_target="tpu_custom_call", output_to_operand_aliasing={{0}: (11, {})} | custom-call | flops 4831838208 | bytes 14000000 | tf_op jit(solution)/shard_map/product/pallas_call | solution.py:208
  111.7 10.5 %all-to-all-start = ((f32[256,1,128]{2,1,0:T(1,128)}), f32[256,1,128]{2,1,0:T(1,128)S(1)}, u32[]{:S(2)}, u32[]{:S(2)}) async-start(f32[256,1,128]{2,1,0:T(1,128)} %bitcast.12), calls=%async_computation | async-start | bytes 262144 | tf_op jit(solution)/shard_map/all_to_all | solution.py:284
  122.2 0.5 slice.221
  123.4 11.8 %all-to-all-done = f32[256,1,128]{2,1,0:T(1,128)S(1)} async-done(((f32[256,1,128]{2,1,0:T(1,128)}), f32[256,1,128]{2,1,0:T(1,128)S(1)}, u32[]{:S(2)}, u32[]{:S(2)}) %all-to-all-start) | async-done | bytes 131104 | tf_op jit(solution)/shard_map/all_to_all | solution.py:284
  135.2 0.6 slice_reduce_fusion
  (68 shorter events, 2.6 us)
Async XLA Ops:
  7.2 83.1 %all-gather.2.cloned.1.call-start = ((), (), s32[]{:S(2)}) async-start(), calls=%async_computation.1 | async-start | bytes 3981312 | tf_op jit(solution)/shard_map/all_gather | solution.py:257
  8.6 11.9 %collective-permute-start.3 = (bf16[72,1024]{1,0:T(8,128)(2,1)S(1)}, bf16[72,1024]{1,0:T(8,128)(2,1)S(1)}, u32[]{:S(2)}, u32[]{:S(2)}) collective-permute-start(bf16[72,1024]{1,0:T(8,128)(2,1)S(1)} %slice.180.refs_0_), channel_id=1, source_target_pairs={{0,64},{32,96},{64,128},{96,160},{128,192},{160,224},{192,0},{224,... | collective-permute-start | bytes 442376 | tf_op jit(solution)/shard_map/ppermute | solution.py:31
  12.5 11.2 %collective-permute-start.2 = (bf16[72,1024]{1,0:T(8,128)(2,1)S(1)}, bf16[72,1024]{1,0:T(8,128)(2,1)S(1)}, u32[]{:S(2)}, u32[]{:S(2)}) collective-permute-start(bf16[72,1024]{1,0:T(8,128)(2,1)S(1)} %slice.180.refs_0_), channel_id=1, source_target_pairs={{0,192},{32,224},{64,0},{96,32},{128,64},{160,96},{192,128},{224,1... | collective-permute-start | bytes 442376 | tf_op jit(solution)/shard_map/ppermute | solution.py:31
  15.7 9.0 %collective-permute-start.23 = (bf16[72,768]{1,0:T(8,128)(2,1)S(1)}, bf16[72,768]{1,0:T(8,128)(2,1)S(1)}, u32[]{:S(2)}, u32[]{:S(2)}) collective-permute-start(bf16[72,768]{1,0:T(8,128)(2,1)S(1)} %slice.219), channel_id=1, source_target_pairs={{0,8},{8,16},{16,24},{24,0},{1,9},{9,17},{17,25},{25,1},{2,10},{10... | collective-permute-start | bytes 331784 | tf_op jit(solution)/shard_map/ppermute | solution.py:31
  17.0 7.8 %collective-permute-start.22 = (bf16[72,768]{1,0:T(8,128)(2,1)S(1)}, bf16[72,768]{1,0:T(8,128)(2,1)S(1)}, u32[]{:S(2)}, u32[]{:S(2)}) collective-permute-start(bf16[72,768]{1,0:T(8,128)(2,1)S(1)} %slice.219), channel_id=1, source_target_pairs={{0,16},{8,24},{16,0},{24,8},{1,17},{9,25},{17,1},{25,9},{2,18},{10... | collective-permute-start | bytes 331784 | tf_op jit(solution)/shard_map/ppermute | solution.py:31
  19.4 5.3 %collective-permute-start.21 = (bf16[72,768]{1,0:T(8,128)(2,1)S(1)}, bf16[72,768]{1,0:T(8,128)(2,1)S(1)}, u32[]{:S(2)}, u32[]{:S(2)}) collective-permute-start(bf16[72,768]{1,0:T(8,128)(2,1)S(1)} %slice.219), channel_id=1, source_target_pairs={{0,24},{8,0},{16,8},{24,16},{1,25},{9,1},{17,9},{25,17},{2,26},{10... | collective-permute-start | bytes 331784 | tf_op jit(solution)/shard_map/ppermute | solution.py:31
  20.6 6.7 %collective-permute-start.5 = (bf16[72,1024]{1,0:T(8,128)(2,1)S(1)}, bf16[72,1024]{1,0:T(8,128)(2,1)S(1)}, u32[]{:S(2)}, u32[]{:S(2)}) collective-permute-start(bf16[72,1024]{1,0:T(8,128)(2,1)S(1)} %collective-permute-done.3.refs_4_), channel_id=1, source_target_pairs={{0,32},{32,64},{64,96},{96,128},{128,160},{160,192},{192,224},{224... | collective-permute-start | bytes 442376 | tf_op jit(solution)/shard_map/ppermute | solution.py:31
  23.7 4.4 %collective-permute-start.4 = (bf16[72,1024]{1,0:T(8,128)(2,1)S(1)}, bf16[72,1024]{1,0:T(8,128)(2,1)S(1)}, u32[]{:S(2)}, u32[]{:S(2)}) collective-permute-start(bf16[72,1024]{1,0:T(8,128)(2,1)S(1)} %collective-permute-done.2.refs_3_), channel_id=1, source_target_pairs={{0,224},{32,0},{64,32},{96,64},{128,96},{160,128},{192,160},{224,1... | collective-permute-start | bytes 442376 | tf_op jit(solution)/shard_map/ppermute | solution.py:31
  28.1 13.5 %collective-permute-start.1 = (bf16[72,1024]{1,0:T(8,128)(2,1)S(1)}, bf16[72,1024]{1,0:T(8,128)(2,1)S(1)}, u32[]{:S(2)}, u32[]{:S(2)}) collective-permute-start(bf16[72,1024]{1,0:T(8,128)(2,1)S(1)} %slice.180.refs_0_), channel_id=1, source_target_pairs={{0,32},{32,64},{64,96},{96,128},{128,160},{160,192},{192,224},{224... | collective-permute-start | bytes 442376 | tf_op jit(solution)/shard_map/ppermute | solution.py:31
  30.1 11.6 %collective-permute-start = (bf16[72,1024]{1,0:T(8,128)(2,1)S(1)}, bf16[72,1024]{1,0:T(8,128)(2,1)S(1)}, u32[]{:S(2)}, u32[]{:S(2)}) collective-permute-start(bf16[72,1024]{1,0:T(8,128)(2,1)S(1)} %slice.180.refs_0_), channel_id=1, source_target_pairs={{0,224},{32,0},{64,32},{96,64},{128,96},{160,128},{192,160},{224,1... | collective-permute-start | bytes 442376 | tf_op jit(solution)/shard_map/ppermute | solution.py:31
  30.9 39.9 %copy-start = (bf16[1024,2304]{1,0:T(8,128)(2,1)S(1)}, bf16[1024,2304]{1,0:T(8,128)(2,1)}, u32[]{:S(2)}) copy-start(bf16[1024,2304]{1,0:T(8,128)(2,1)} %refs_1_.1) | copy-start | bytes 14155780
  32.6 9.1 %collective-permute-start.6 = (bf16[72,1024]{1,0:T(8,128)(2,1)S(1)}, bf16[72,1024]{1,0:T(8,128)(2,1)S(1)}, u32[]{:S(2)}, u32[]{:S(2)}) collective-permute-start(bf16[72,1024]{1,0:T(8,128)(2,1)S(1)} %collective-permute-done.2.refs_3_), channel_id=1, source_target_pairs={{0,192},{32,224},{64,0},{96,32},{128,64},{160,96},{192,128},{224,1... | collective-permute-start | bytes 442376 | tf_op jit(solution)/shard_map/ppermute | solution.py:31
  34.3 0.7 copy-start.7
  39.8 1.9 %copy-start.8 = (bf16[4,448,1024]{2,1,0:T(8,128)(2,1)}, bf16[4,448,1024]{2,1,0:T(8,128)(2,1)S(1)}, u32[]{:S(2)}) copy-start(bf16[4,448,1024]{2,1,0:T(8,128)(2,1)S(1)} %get-tuple-element.35) | copy-start | bytes 11010052
  41.7 8.9 %collective-permute-start.13 = (f32[4,8,448]{2,1,0:T(8,128)S(1)}, f32[4,8,448]{2,1,0:T(8,128)S(1)}, u32[]{:S(2)}, u32[]{:S(2)}) collective-permute-start(f32[4,8,448]{2,1,0:T(8,128)S(1)} %get-tuple-element.36), channel_id=1, source_target_pairs={{0,16},{8,24},{16,0},{24,8},{1,17},{9,25},{17,1},{25,9},{2,18},{10... | collective-permute-start | bytes 172040 | tf_op jit(solution)/shard_map/ppermute | solution.py:31
  44.5 6.1 %collective-permute-start.12 = (f32[4,8,448]{2,1,0:T(8,128)S(1)}, f32[4,8,448]{2,1,0:T(8,128)S(1)}, u32[]{:S(2)}, u32[]{:S(2)}) collective-permute-start(f32[4,8,448]{2,1,0:T(8,128)S(1)} %get-tuple-element.36), channel_id=1, source_target_pairs={{0,8},{8,16},{16,24},{24,0},{1,9},{9,17},{17,25},{25,1},{2,10},{10... | collective-permute-start | bytes 172040 | tf_op jit(solution)/shard_map/ppermute | solution.py:31
  44.8 5.8 %collective-permute-start.11 = (f32[4,8,448]{2,1,0:T(8,128)S(1)}, f32[4,8,448]{2,1,0:T(8,128)S(1)}, u32[]{:S(2)}, u32[]{:S(2)}) collective-permute-start(f32[4,8,448]{2,1,0:T(8,128)S(1)} %get-tuple-element.36), channel_id=1, source_target_pairs={{0,24},{8,0},{16,8},{24,16},{1,25},{9,1},{17,9},{25,17},{2,26},{10... | collective-permute-start | bytes 172040 | tf_op jit(solution)/shard_map/ppermute | solution.py:31
  47.8 29.0 %collective-permute-start.8 = (bf16[576,1024]{1,0:T(8,128)(2,1)S(1)}, bf16[576,1024]{1,0:T(8,128)(2,1)S(1)}, u32[]{:S(2)}, u32[]{:S(2)}) collective-permute-start(bf16[576,1024]{1,0:T(8,128)(2,1)S(1)} %bitcast.43), channel_id=1, source_target_pairs={{0,8},{8,16},{16,24},{24,0},{1,9},{9,17},{17,25},{25,1},{2,10},{10... | collective-permute-start | bytes 3538952 | tf_op jit(solution)/shard_map/ppermute | solution.py:31
  47.9 29.8 %collective-permute-start.7 = (bf16[576,1024]{1,0:T(8,128)(2,1)S(1)}, bf16[576,1024]{1,0:T(8,128)(2,1)S(1)}, u32[]{:S(2)}, u32[]{:S(2)}) collective-permute-start(bf16[576,1024]{1,0:T(8,128)(2,1)S(1)} %bitcast.44), channel_id=1, source_target_pairs={{0,24},{8,0},{16,8},{24,16},{1,25},{9,1},{17,9},{25,17},{2,26},{10... | collective-permute-start | bytes 3538952 | tf_op jit(solution)/shard_map/ppermute | solution.py:31
  50.8 8.7 %collective-permute-start.20 = (f32[4,8,448]{2,1,0:T(8,128)S(1)}, f32[4,8,448]{2,1,0:T(8,128)S(1)}, u32[]{:S(2)}, u32[]{:S(2)}) collective-permute-start(f32[4,8,448]{2,1,0:T(8,128)S(1)} %select_select_fusion.1), channel_id=1, source_target_pairs={{0,128},{32,160},{64,192},{96,224},{128,0},{160,32},{192,64},{224,... | collective-permute-start | bytes 172040 | tf_op jit(solution)/shard_map/ppermute | solution.py:31
  55.0 9.9 %collective-permute-start.19 = (f32[4,8,448]{2,1,0:T(8,128)S(1)}, f32[4,8,448]{2,1,0:T(8,128)S(1)}, u32[]{:S(2)}, u32[]{:S(2)}) collective-permute-start(f32[4,8,448]{2,1,0:T(8,128)S(1)} %select_select_fusion.1), channel_id=1, source_target_pairs={{0,96},{32,128},{64,160},{96,192},{128,224},{160,0},{192,32},{224,... | collective-permute-start | bytes 172040 | tf_op jit(solution)/shard_map/ppermute | solution.py:31
  55.2 10.9 %collective-permute-start.18 = (f32[4,8,448]{2,1,0:T(8,128)S(1)}, f32[4,8,448]{2,1,0:T(8,128)S(1)}, u32[]{:S(2)}, u32[]{:S(2)}) collective-permute-start(f32[4,8,448]{2,1,0:T(8,128)S(1)} %select_select_fusion.1), channel_id=1, source_target_pairs={{0,160},{32,192},{64,224},{96,0},{128,32},{160,64},{192,96},{224,1... | collective-permute-start | bytes 172040 | tf_op jit(solution)/shard_map/ppermute | solution.py:31
  59.5 10.4 %collective-permute-start.17 = (f32[4,8,448]{2,1,0:T(8,128)S(1)}, f32[4,8,448]{2,1,0:T(8,128)S(1)}, u32[]{:S(2)}, u32[]{:S(2)}) collective-permute-start(f32[4,8,448]{2,1,0:T(8,128)S(1)} %select_select_fusion.1), channel_id=1, source_target_pairs={{0,64},{32,96},{64,128},{96,160},{128,192},{160,224},{192,0},{224,... | collective-permute-start | bytes 172040 | tf_op jit(solution)/shard_map/ppermute | solution.py:31
  65.0 11.5 %collective-permute-start.16 = (f32[4,8,448]{2,1,0:T(8,128)S(1)}, f32[4,8,448]{2,1,0:T(8,128)S(1)}, u32[]{:S(2)}, u32[]{:S(2)}) collective-permute-start(f32[4,8,448]{2,1,0:T(8,128)S(1)} %select_select_fusion.1), channel_id=1, source_target_pairs={{0,192},{32,224},{64,0},{96,32},{128,64},{160,96},{192,128},{224,1... | collective-permute-start | bytes 172040 | tf_op jit(solution)/shard_map/ppermute | solution.py:31
  66.1 10.3 %collective-permute-start.15 = (f32[4,8,448]{2,1,0:T(8,128)S(1)}, f32[4,8,448]{2,1,0:T(8,128)S(1)}, u32[]{:S(2)}, u32[]{:S(2)}) collective-permute-start(f32[4,8,448]{2,1,0:T(8,128)S(1)} %select_select_fusion.1), channel_id=1, source_target_pairs={{0,32},{32,64},{64,96},{96,128},{128,160},{160,192},{192,224},{224... | collective-permute-start | bytes 172040 | tf_op jit(solution)/shard_map/ppermute | solution.py:31
  69.9 6.5 %collective-permute-start.14 = (f32[4,8,448]{2,1,0:T(8,128)S(1)}, f32[4,8,448]{2,1,0:T(8,128)S(1)}, u32[]{:S(2)}, u32[]{:S(2)}) collective-permute-start(f32[4,8,448]{2,1,0:T(8,128)S(1)} %select_select_fusion.1), channel_id=1, source_target_pairs={{0,224},{32,0},{64,32},{96,64},{128,96},{160,128},{192,160},{224,1... | collective-permute-start | bytes 172040 | tf_op jit(solution)/shard_map/ppermute | solution.py:31
  74.3 2.1 %copy-start.2 = (bf16[1024,2304]{1,0:T(8,128)(2,1)}, bf16[1024,2304]{1,0:T(8,128)(2,1)S(1)}, u32[]{:S(2)}) copy-start(bf16[1024,2304]{1,0:T(8,128)(2,1)S(1)} %columns_by_x.1.refs_1_) | copy-start | bytes 14155780
  76.8 1.3 copy-start.3
  77.7 23.3 %collective-permute-start.10 = (bf16[576,512]{1,0:T(8,128)(2,1)}, bf16[576,512]{1,0:T(8,128)(2,1)S(1)}, u32[]{:S(2)}, u32[]{:S(2)}) collective-permute-start(bf16[576,512]{1,0:T(8,128)(2,1)} %slice.182), channel_id=1, source_target_pairs={{0,8},{8,16},{16,24},{24,0},{1,9},{9,17},{17,25},{25,1},{2,10},{10... | collective-permute-start | bytes 1769480 | tf_op jit(solution)/shard_map/ppermute | solution.py:31
  78.1 1.2 copy-start.5
  78.1 23.0 %slice-start = ((s8[4718592]{0:T(1024)(128)(4,1)}), s8[524288]{0:T(1024)(128)(4,1)S(1)}, s32[]{:S(2)}) async-start(s8[4718592]{0:T(1024)(128)(4,1)} %bitcast.41), calls=%async_computation.2 | async-start | bytes 1048576
  79.3 21.8 %collective-permute-start.9 = (bf16[576,512]{1,0:T(8,128)(2,1)}, bf16[576,512]{1,0:T(8,128)(2,1)}, u32[]{:S(2)}, u32[]{:S(2)}) collective-permute-start(bf16[576,512]{1,0:T(8,128)(2,1)} %slice.181), channel_id=1, source_target_pairs={{0,24},{8,0},{16,8},{24,16},{1,25},{9,1},{17,9},{25,17},{2,26},{10... | collective-permute-start | bytes 1769480 | tf_op jit(solution)/shard_map/ppermute | solution.py:31
  90.3 2.3 %copy-start.1 = (bf16[1024,2304]{1,0:T(8,128)(2,1)S(1)}, bf16[1024,2304]{1,0:T(8,128)(2,1)}, u32[]{:S(2)}) copy-start(bf16[1024,2304]{1,0:T(8,128)(2,1)} %refs_1_.1) | copy-start | bytes 14155780
  92.6 8.4 %slice-start.1 = ((s8[4718592]{0:T(1024)(128)(4,1)}), s8[4194304]{0:T(1024)(128)(4,1)S(1)}, s32[]{:S(2)}) async-start(s8[4718592]{0:T(1024)(128)(4,1)} %bitcast.41), calls=%async_computation.3 | async-start | bytes 8388608
  92.6 8.5 %copy-start.4 = (bf16[576,1024]{1,0:T(8,128)(2,1)S(1)}, bf16[576,1024]{1,0:T(8,128)(2,1)}, u32[]{:S(2)}) copy-start(bf16[576,1024]{1,0:T(8,128)(2,1)} %copy-done.3) | copy-start | bytes 3538948
  92.6 8.5 %copy-start.6 = (bf16[576,1024]{1,0:T(8,128)(2,1)S(1)}, bf16[576,1024]{1,0:T(8,128)(2,1)}, u32[]{:S(2)}) copy-start(bf16[576,1024]{1,0:T(8,128)(2,1)} %copy-done.5) | copy-start | bytes 3538948
  111.7 23.4 %all-to-all-start = ((f32[256,1,128]{2,1,0:T(1,128)}), f32[256,1,128]{2,1,0:T(1,128)S(1)}, u32[]{:S(2)}, u32[]{:S(2)}) async-start(f32[256,1,128]{2,1,0:T(1,128)} %bitcast.12), calls=%async_computation | async-start | bytes 262144 | tf_op jit(solution)/shard_map/all_to_all | solution.py:284
Sparse Core Ops, SparseCore 0:
  28.3 61.9 all-gather.1

commit v3 on v2

--- a/solution.py
+++ b/solution.py
@@ -141,12 +141,14 @@
     return lax.dot_general(weights, student, (((0,), (1,)), ((), ())), preferred_element_type=f32)
 
 
-def product_kernel(steps, parts, lefts, first, xs, student, *refs):
+def product_kernel(steps, parts, lefts, first, student, *refs):
     if parts == 1:
         weights = refs[0][...]
         refs = refs[1:]
     else:
         *refs, joined = refs
+        x = lax.axis_index("seq_1")
+        xs = [lax.rem(x + by + NX, NX) for by in X_ORDER]
         for k in range(parts - 1):
             joined[xs[k]] = refs[k][...]
         left = pl.program_id(0) < lefts
@@ -189,31 +191,30 @@
     lefts = weights[-2].shape[1] // BN if parts > 1 else 0
     in_specs = [pl.BlockSpec(memory_space=pltpu.VMEM)]
     whole = len(weights) - 2 if parts > 1 else 1
-    in_specs += [pl.BlockSpec((k, BN), lambda i, p: (0, i))] * whole
+    in_specs += [pl.BlockSpec((k, BN), lambda i: (0, i))] * whole
     if parts > 1:
         in_specs += [
-            pl.BlockSpec((k, BN), lambda i, p: (0, jnp.minimum(i, lefts - 1))),
-            pl.BlockSpec((k, BN), lambda i, p: (0, jnp.maximum(i - lefts, 0))),
+            pl.BlockSpec((k, BN), lambda i: (0, jnp.minimum(i, lefts - 1))),
+            pl.BlockSpec((k, BN), lambda i: (0, jnp.maximum(i - lefts, 0))),
         ]
     in_specs += [
-        pl.BlockSpec((BN, tokens), lambda i, p: (i + at, 0)),
-        pl.BlockSpec((BN, 2), lambda i, p: (i + at, 0)),
-        pl.BlockSpec((1, tokens), lambda i, p: (0, 0)),
+        pl.BlockSpec((BN, tokens), lambda i: (i + at, 0)),
+        pl.BlockSpec((BN, 2), lambda i: (i + at, 0)),
+        pl.BlockSpec((1, tokens), lambda i: (0, 0)),
     ]
-    args = [xs, student, *weights, stay(chosen), scale, weight]
+    args = [student, *weights, stay(chosen), scale, weight]
     if not first:
-        in_specs += [pl.BlockSpec((1, tokens), lambda i, p: (0, 0)), pl.BlockSpec(memory_space=pl.ANY)]
+        in_specs += [pl.BlockSpec((1, tokens), lambda i: (0, 0)), pl.BlockSpec(memory_space=pl.ANY)]
         args += list(before)
     loss = (1, tokens) if first else (copies, 128)
     return pl.pallas_call(
         lambda *refs: product_kernel(steps, parts, lefts, first, *refs),
-        grid_spec=pltpu.PrefetchScalarGridSpec(
-            num_scalar_prefetch=1,
+        grid_spec=pl.GridSpec(
             grid=(steps,),
             in_specs=in_specs,
             out_specs=[
-                pl.BlockSpec((BN, tokens), lambda i, p: (i + at, 0)),
-                pl.BlockSpec(loss, lambda i, p: (0, 0)),
+                pl.BlockSpec((BN, tokens), lambda i: (i + at, 0)),
+                pl.BlockSpec(loss, lambda i: (0, 0)),
             ],
             scratch_shapes=[pltpu.VMEM((1, tokens), f32)] + ([pltpu.VMEM((parts, k, BN), bf16)] if parts > 1 else []),
         ),

time: 145 us -> 144 us (level)
  waiting for transfers between devices: 29.2 us -> 31.8 us
  starting transfers between devices: 53.6 us -> 51.9 us
    ppermute x24, starting transfers between devices: 43.2 us -> 41.3 us  [shift(): lax.ppermute(value, axis, [(i, (i - by) % size) for i in range(size)])]
    ppermute x24, waiting for transfers between devices: 9.29 us -> 10.8 us  [shift(): lax.ppermute(value, axis, [(i, (i - by) % size) for i in range(size)])]
where the time goes in v3:
time: 144 us; the launch traced here: 143 us
  starting transfers between devices  51.9 us (36%)
  waiting for transfers between devices  31.8 us (22%)
  Pallas kernels  26.8 us (19%)
  between operations  16.7 us (12%)
  local copies, waits for them, and re-layouts  12.4 us (9%)
  other arithmetic  3.74 us (3%)
    ppermute x24, starting transfers between devices, shift(): lax.ppermute(value, axis, [(i, (i - by) % size) for i in range(size)])  41.3 us
    pallas_call x2, Pallas kernels, product(): pl.pallas_call(lambda *refs: product_kernel(steps, parts, lefts, first, *...  17.9 us
    all_to_all x1, waiting for transfers between devices, shards(): squares = jnp.sum(lax.all_to_all(loss, ALL, 0, 0, tiled=True)[:, 0])  11.8 us
    ppermute x24, waiting for transfers between devices, shift(): lax.ppermute(value, axis, [(i, (i - by) % size) for i in range(size)])  10.8 us
    all_to_all x1, starting transfers between devices, shards(): squares = jnp.sum(lax.all_to_all(loss, ALL, 0, 0, tiled=True)[:, 0])  10.5 us
    all_gather x1, waiting for transfers between devices, shards(): lax.all_gather(after(c_block, *[line[k] for k in SC_AFTER]), 'seq_0', axi...  9.2 us
    unnamed x27, local copies, waits for them, and re-layouts  7.69 us
    pallas_call x1, Pallas kernels, local_moments(): pl.pallas_call(moments_kernel, grid_spec=pltpu.PrefetchScalarGridSpec(num...  4.81 us
  transfers between devices with their start and end apart: 26, of which 7 were waited for; matrix products, arithmetic and copies ran while one was open for 5% of the time, Pallas kernels for 12%

profile of v3, /device:TPU:1, one launch (start us, length us, event | category | flops | bytes accessed | tf_op | source)
XLA Modules:
  0.0 143.4 jit_solution(2569207294707958192)
XLA Ops:
  7.2 1.1 copy.17
  8.3 0.3 reshape.92
  8.6 3.9 %collective-permute-start.3 = (bf16[72,1024]{1,0:T(8,128)(2,1)S(1)}, bf16[72,1024]{1,0:T(8,128)(2,1)S(1)}, u32[]{:S(2)}, u32[]{:S(2)}) collective-permute-start(bf16[72,1024]{1,0:T(8,128)(2,1)S(1)} %slice.180.refs_0_), channel_id=1, source_target_pairs={{0,64},{32,96},{64,128},{96,160},{128,192},{160,224},{192,0},{224,... | collective-permute-start | bytes 442376 | tf_op jit(solution)/shard_map/ppermute | solution.py:31
  12.5 3.1 %collective-permute-start.2 = (bf16[72,1024]{1,0:T(8,128)(2,1)S(1)}, bf16[72,1024]{1,0:T(8,128)(2,1)S(1)}, u32[]{:S(2)}, u32[]{:S(2)}) collective-permute-start(bf16[72,1024]{1,0:T(8,128)(2,1)S(1)} %slice.180.refs_0_), channel_id=1, source_target_pairs={{0,192},{32,224},{64,0},{96,32},{128,64},{160,96},{192,128},{224,1... | collective-permute-start | bytes 442376 | tf_op jit(solution)/shard_map/ppermute | solution.py:31
  15.7 1.3 collective-permute-start.23
  17.0 2.5 %collective-permute-start.22 = (bf16[72,768]{1,0:T(8,128)(2,1)S(1)}, bf16[72,768]{1,0:T(8,128)(2,1)S(1)}, u32[]{:S(2)}, u32[]{:S(2)}) collective-permute-start(bf16[72,768]{1,0:T(8,128)(2,1)S(1)} %slice.219), channel_id=1, source_target_pairs={{0,16},{8,24},{16,0},{24,8},{1,17},{9,25},{17,1},{25,9},{2,18},{10... | collective-permute-start | bytes 331784 | tf_op jit(solution)/shard_map/ppermute | solution.py:31
  19.4 1.2 collective-permute-start.21
  20.6 2.8 %collective-permute-start.5 = (bf16[72,1024]{1,0:T(8,128)(2,1)S(1)}, bf16[72,1024]{1,0:T(8,128)(2,1)S(1)}, u32[]{:S(2)}, u32[]{:S(2)}) collective-permute-start(bf16[72,1024]{1,0:T(8,128)(2,1)S(1)} %collective-permute-done.3.refs_4_), channel_id=1, source_target_pairs={{0,32},{32,64},{64,96},{96,128},{128,160},{160,192},{192,224},{224... | collective-permute-start | bytes 442376 | tf_op jit(solution)/shard_map/ppermute | solution.py:31
  23.3 0.4 collective-permute-done.2.refs_3_
  23.7 0.5 collective-permute-start.4
  24.7 1.0 fusion.1
  25.7 1.5 %collective-permute-done.5.refs_6_ = bf16[72,1024]{1,0:T(8,128)(2,1)S(1)} collective-permute-done((bf16[72,1024]{1,0:T(8,128)(2,1)S(1)}, bf16[72,1024]{1,0:T(8,128)(2,1)S(1)}, u32[]{:S(2)}, u32[]{:S(2)}) %collective-permute-start.5) | collective-permute-done | bytes 147488 | tf_op jit(solution)/shard_map/ppermute | solution.py:31
  27.2 0.9 collective-permute-done.4.refs_5_
  28.1 2.0 %collective-permute-start.1 = (bf16[72,1024]{1,0:T(8,128)(2,1)S(1)}, bf16[72,1024]{1,0:T(8,128)(2,1)S(1)}, u32[]{:S(2)}, u32[]{:S(2)}) collective-permute-start(bf16[72,1024]{1,0:T(8,128)(2,1)S(1)} %slice.180.refs_0_), channel_id=1, source_target_pairs={{0,32},{32,64},{64,96},{96,128},{128,160},{160,192},{192,224},{224... | collective-permute-start | bytes 442376 | tf_op jit(solution)/shard_map/ppermute | solution.py:31
  30.1 0.8 collective-permute-start
  30.9 0.8 convert_element_type.3
  31.7 1.0 collective-permute-start.6
  32.8 0.7 and_select_fusion.1.zs
  33.5 0.7 copy-done.7
  34.1 4.8 %moments.1 = (bf16[4,448,1024]{2,1,0:T(8,128)(2,1)S(1)}, f32[4,8,448]{2,1,0:T(8,128)S(1)}) custom-call(s32[4]{0:T(128)S(1)} %copy-done.7, bf16[4,448,1024]{2,1,0:T(8,128)(2,1)} %bitcast.51, f32[1,1024]{1,0:T(1,128)S(1)} %bitcast.46), custom_call_target="tpu_custom_call" | custom-call | flops 20000000 | bytes 8000000 | tf_op jit(solution)/shard_map/moments/pallas_call | solution.py:66
  38.9 1.9 %copy-done.8 = bf16[4,448,1024]{2,1,0:T(8,128)(2,1)} copy-done((bf16[4,448,1024]{2,1,0:T(8,128)(2,1)}, bf16[4,448,1024]{2,1,0:T(8,128)(2,1)S(1)}, u32[]{:S(2)}) %copy-start.8) | copy-done | bytes 3670040
  40.8 2.8 %collective-permute-start.13 = (f32[4,8,448]{2,1,0:T(8,128)S(1)}, f32[4,8,448]{2,1,0:T(8,128)S(1)}, u32[]{:S(2)}, u32[]{:S(2)}) collective-permute-start(f32[4,8,448]{2,1,0:T(8,128)S(1)} %get-tuple-element.34), channel_id=1, source_target_pairs={{0,16},{8,24},{16,0},{24,8},{1,17},{9,25},{17,1},{25,9},{2,18},{10... | collective-permute-start | bytes 172040 | tf_op jit(solution)/shard_map/ppermute | solution.py:31
  43.7 0.3 collective-permute-start.12
  44.0 2.4 %collective-permute-start.11 = (f32[4,8,448]{2,1,0:T(8,128)S(1)}, f32[4,8,448]{2,1,0:T(8,128)S(1)}, u32[]{:S(2)}, u32[]{:S(2)}) collective-permute-start(f32[4,8,448]{2,1,0:T(8,128)S(1)} %get-tuple-element.34), channel_id=1, source_target_pairs={{0,24},{8,0},{16,8},{24,16},{1,25},{9,1},{17,9},{25,17},{2,26},{10... | collective-permute-start | bytes 172040 | tf_op jit(solution)/shard_map/ppermute | solution.py:31
  46.3 0.6 placed.1
  47.1 2.7 %collective-permute-start.7 = (bf16[576,1024]{1,0:T(8,128)(2,1)S(1)}, bf16[576,1024]{1,0:T(8,128)(2,1)S(1)}, u32[]{:S(2)}, u32[]{:S(2)}) collective-permute-start(bf16[576,1024]{1,0:T(8,128)(2,1)S(1)} %bitcast.44), channel_id=1, source_target_pairs={{0,24},{8,0},{16,8},{24,16},{1,25},{9,1},{17,9},{25,17},{2,26},{10... | collective-permute-start | bytes 3538952 | tf_op jit(solution)/shard_map/ppermute | solution.py:31
  50.0 4.2 %collective-permute-start.20 = (f32[4,8,448]{2,1,0:T(8,128)S(1)}, f32[4,8,448]{2,1,0:T(8,128)S(1)}, u32[]{:S(2)}, u32[]{:S(2)}) collective-permute-start(f32[4,8,448]{2,1,0:T(8,128)S(1)} %select_select_fusion.1), channel_id=1, source_target_pairs={{0,128},{32,160},{64,192},{96,224},{128,0},{160,32},{192,64},{224,... | collective-permute-start | bytes 172040 | tf_op jit(solution)/shard_map/ppermute | solution.py:31
  54.3 4.3 %collective-permute-start.18 = (f32[4,8,448]{2,1,0:T(8,128)S(1)}, f32[4,8,448]{2,1,0:T(8,128)S(1)}, u32[]{:S(2)}, u32[]{:S(2)}) collective-permute-start(f32[4,8,448]{2,1,0:T(8,128)S(1)} %select_select_fusion.1), channel_id=1, source_target_pairs={{0,160},{32,192},{64,224},{96,0},{128,32},{160,64},{192,96},{224,1... | collective-permute-start | bytes 172040 | tf_op jit(solution)/shard_map/ppermute | solution.py:31
  58.7 1.9 %collective-permute-start.17 = (f32[4,8,448]{2,1,0:T(8,128)S(1)}, f32[4,8,448]{2,1,0:T(8,128)S(1)}, u32[]{:S(2)}, u32[]{:S(2)}) collective-permute-start(f32[4,8,448]{2,1,0:T(8,128)S(1)} %select_select_fusion.1), channel_id=1, source_target_pairs={{0,64},{32,96},{64,128},{96,160},{128,192},{160,224},{192,0},{224,... | collective-permute-start | bytes 172040 | tf_op jit(solution)/shard_map/ppermute | solution.py:31
  60.6 3.6 %collective-permute-done.19 = f32[4,8,448]{2,1,0:T(8,128)S(1)} collective-permute-done((f32[4,8,448]{2,1,0:T(8,128)S(1)}, f32[4,8,448]{2,1,0:T(8,128)S(1)}, u32[]{:S(2)}, u32[]{:S(2)}) %collective-permute-start.19) | collective-permute-done | bytes 57376 | tf_op jit(solution)/shard_map/ppermute | solution.py:31
  64.5 0.7 collective-permute-start.15
  65.2 4.3 %collective-permute-done.17 = f32[4,8,448]{2,1,0:T(8,128)S(1)} collective-permute-done((f32[4,8,448]{2,1,0:T(8,128)S(1)}, f32[4,8,448]{2,1,0:T(8,128)S(1)}, u32[]{:S(2)}, u32[]{:S(2)}) %collective-permute-start.17) | collective-permute-done | bytes 57376 | tf_op jit(solution)/shard_map/ppermute | solution.py:31
  69.7 3.4 %columns_by_x.1.refs_0_ = bf16[1024,2304]{1,0:T(8,128)(2,1)S(1)} custom-call(bf16[1024,2304]{1,0:T(8,128)(2,1)S(1)} %copy-done), custom_call_target="tpu_custom_call" | custom-call | bytes 10000000 | tf_op jit(solution)/shard_map/columns_by_x/pallas_call | solution.py:128
  73.1 2.1 %copy-done.2 = bf16[1024,2304]{1,0:T(8,128)(2,1)} copy-done((bf16[1024,2304]{1,0:T(8,128)(2,1)}, bf16[1024,2304]{1,0:T(8,128)(2,1)S(1)}, u32[]{:S(2)}) %copy-start.2) | copy-done | bytes 4718616
  75.6 0.9 slice.182
  76.6 0.3 copy-done.3
  76.9 0.9 slice.181
  77.8 0.3 copy-done.5
  78.1 2.4 %collective-permute-start.9 = (bf16[576,512]{1,0:T(8,128)(2,1)}, bf16[576,512]{1,0:T(8,128)(2,1)}, u32[]{:S(2)}, u32[]{:S(2)}) collective-permute-start(bf16[576,512]{1,0:T(8,128)(2,1)} %slice.181), channel_id=1, source_target_pairs={{0,24},{8,0},{16,8},{24,16},{1,25},{9,1},{17,9},{25,17},{2,26},{10... | collective-permute-start | bytes 1769480 | tf_op jit(solution)/shard_map/ppermute | solution.py:31
  80.7 0.3 copy.19.refs_3_.refs_7_
  81.1 9.2 %all-gather.2.cloned.1.call-done.refs_1_ = bf16[2304,768]{1,0:T(8,128)(2,1)} async-done(((bf16[288,768]{1,0:T(8,128)(2,1)}), bf16[2304,768]{1,0:T(8,128)(2,1)}) %all-gather.2.cloned.1.call-update) | async-done | bytes 3538960 | tf_op jit(solution)/shard_map/all_gather | solution.py:258
  90.3 2.3 %copy-done.1 = bf16[1024,2304]{1,0:T(8,128)(2,1)S(1)} copy-done((bf16[1024,2304]{1,0:T(8,128)(2,1)S(1)}, bf16[1024,2304]{1,0:T(8,128)(2,1)}, u32[]{:S(2)}) %copy-start.1) | copy-done | bytes 4718616
  92.6 7.8 %product.2 = (bf16[1792,1024]{1,0:T(8,128)(2,1)}, f32[1,1024]{1,0:T(1,128)S(1)}) custom-call(bf16[1024,2304]{1,0:T(8,128)(2,1)S(1)} %copy-done.1, bf16[2304,768]{1,0:T(8,128)(2,1)} %all-gather.2.cloned.1.call-done.refs_1_, bf16[1792,1024]{1,0:T(8,128)(2,1)} %bitcast.49, f32[1792,2]{1,0:T(8,128)S(1)} %copy.19.refs_3_.refs_7_, f32[1,1024]{1,0:T(1,128)S(1)} %bitcast.47), custom_call_target="tpu_custom_call" | custom-call | flops 3623878656 | bytes 14000000 | tf_op jit(solution)/shard_map/product/pallas_call | solution.py:210
  100.4 10.2 %product.3 = (bf16[1792,1024]{1,0:T(8,128)(2,1)}, f32[256,128]{1,0:T(8,128)}) custom-call(bf16[1024,2304]{1,0:T(8,128)(2,1)S(1)} %bitcast.42, bf16[576,1024]{1,0:T(8,128)(2,1)S(1)} %bitcast.45, bf16[576,1024]{1,0:T(8,128)(2,1)S(1)} %copy-done.6, bf16[576,1024]{1,0:T(8,128)(2,1)S(1)} %copy-done.4, ...), custom_call_target="tpu_custom_call", output_to_operand_aliasing={{0}: (10, {})} | custom-call | flops 4831838208 | bytes 14000000 | tf_op jit(solution)/shard_map/product/pallas_call | solution.py:210
  110.6 10.5 %all-to-all-start = ((f32[256,1,128]{2,1,0:T(1,128)}), f32[256,1,128]{2,1,0:T(1,128)S(1)}, u32[]{:S(2)}, u32[]{:S(2)}) async-start(f32[256,1,128]{2,1,0:T(1,128)} %bitcast.12), calls=%async_computation | async-start | bytes 262144 | tf_op jit(solution)/shard_map/all_to_all | solution.py:285
  121.1 0.5 slice.221
  122.3 11.8 %all-to-all-done = f32[256,1,128]{2,1,0:T(1,128)S(1)} async-done(((f32[256,1,128]{2,1,0:T(1,128)}), f32[256,1,128]{2,1,0:T(1,128)S(1)}, u32[]{:S(2)}, u32[]{:S(2)}) %all-to-all-start) | async-done | bytes 131104 | tf_op jit(solution)/shard_map/all_to_all | solution.py:285
  134.1 0.6 slice_reduce_fusion
  (67 shorter events, 2.2 us)
Async XLA Ops:
  7.2 83.1 %all-gather.2.cloned.1.call-start = ((), (), s32[]{:S(2)}) async-start(), calls=%async_computation.1 | async-start | bytes 3981312 | tf_op jit(solution)/shard_map/all_gather | solution.py:258
  8.6 11.9 %collective-permute-start.3 = (bf16[72,1024]{1,0:T(8,128)(2,1)S(1)}, bf16[72,1024]{1,0:T(8,128)(2,1)S(1)}, u32[]{:S(2)}, u32[]{:S(2)}) collective-permute-start(bf16[72,1024]{1,0:T(8,128)(2,1)S(1)} %slice.180.refs_0_), channel_id=1, source_target_pairs={{0,64},{32,96},{64,128},{96,160},{128,192},{160,224},{192,0},{224,... | collective-permute-start | bytes 442376 | tf_op jit(solution)/shard_map/ppermute | solution.py:31
  12.5 11.2 %collective-permute-start.2 = (bf16[72,1024]{1,0:T(8,128)(2,1)S(1)}, bf16[72,1024]{1,0:T(8,128)(2,1)S(1)}, u32[]{:S(2)}, u32[]{:S(2)}) collective-permute-start(bf16[72,1024]{1,0:T(8,128)(2,1)S(1)} %slice.180.refs_0_), channel_id=1, source_target_pairs={{0,192},{32,224},{64,0},{96,32},{128,64},{160,96},{192,128},{224,1... | collective-permute-start | bytes 442376 | tf_op jit(solution)/shard_map/ppermute | solution.py:31
  15.7 9.0 %collective-permute-start.23 = (bf16[72,768]{1,0:T(8,128)(2,1)S(1)}, bf16[72,768]{1,0:T(8,128)(2,1)S(1)}, u32[]{:S(2)}, u32[]{:S(2)}) collective-permute-start(bf16[72,768]{1,0:T(8,128)(2,1)S(1)} %slice.219), channel_id=1, source_target_pairs={{0,8},{8,16},{16,24},{24,0},{1,9},{9,17},{17,25},{25,1},{2,10},{10... | collective-permute-start | bytes 331784 | tf_op jit(solution)/shard_map/ppermute | solution.py:31
  17.0 7.8 %collective-permute-start.22 = (bf16[72,768]{1,0:T(8,128)(2,1)S(1)}, bf16[72,768]{1,0:T(8,128)(2,1)S(1)}, u32[]{:S(2)}, u32[]{:S(2)}) collective-permute-start(bf16[72,768]{1,0:T(8,128)(2,1)S(1)} %slice.219), channel_id=1, source_target_pairs={{0,16},{8,24},{16,0},{24,8},{1,17},{9,25},{17,1},{25,9},{2,18},{10... | collective-permute-start | bytes 331784 | tf_op jit(solution)/shard_map/ppermute | solution.py:31
  19.4 5.3 %collective-permute-start.21 = (bf16[72,768]{1,0:T(8,128)(2,1)S(1)}, bf16[72,768]{1,0:T(8,128)(2,1)S(1)}, u32[]{:S(2)}, u32[]{:S(2)}) collective-permute-start(bf16[72,768]{1,0:T(8,128)(2,1)S(1)} %slice.219), channel_id=1, source_target_pairs={{0,24},{8,0},{16,8},{24,16},{1,25},{9,1},{17,9},{25,17},{2,26},{10... | collective-permute-start | bytes 331784 | tf_op jit(solution)/shard_map/ppermute | solution.py:31
  20.6 6.7 %collective-permute-start.5 = (bf16[72,1024]{1,0:T(8,128)(2,1)S(1)}, bf16[72,1024]{1,0:T(8,128)(2,1)S(1)}, u32[]{:S(2)}, u32[]{:S(2)}) collective-permute-start(bf16[72,1024]{1,0:T(8,128)(2,1)S(1)} %collective-permute-done.3.refs_4_), channel_id=1, source_target_pairs={{0,32},{32,64},{64,96},{96,128},{128,160},{160,192},{192,224},{224... | collective-permute-start | bytes 442376 | tf_op jit(solution)/shard_map/ppermute | solution.py:31
  23.7 4.4 %collective-permute-start.4 = (bf16[72,1024]{1,0:T(8,128)(2,1)S(1)}, bf16[72,1024]{1,0:T(8,128)(2,1)S(1)}, u32[]{:S(2)}, u32[]{:S(2)}) collective-permute-start(bf16[72,1024]{1,0:T(8,128)(2,1)S(1)} %collective-permute-done.2.refs_3_), channel_id=1, source_target_pairs={{0,224},{32,0},{64,32},{96,64},{128,96},{160,128},{192,160},{224,1... | collective-permute-start | bytes 442376 | tf_op jit(solution)/shard_map/ppermute | solution.py:31
  28.1 12.7 %collective-permute-start.1 = (bf16[72,1024]{1,0:T(8,128)(2,1)S(1)}, bf16[72,1024]{1,0:T(8,128)(2,1)S(1)}, u32[]{:S(2)}, u32[]{:S(2)}) collective-permute-start(bf16[72,1024]{1,0:T(8,128)(2,1)S(1)} %slice.180.refs_0_), channel_id=1, source_target_pairs={{0,32},{32,64},{64,96},{96,128},{128,160},{160,192},{192,224},{224... | collective-permute-start | bytes 442376 | tf_op jit(solution)/shard_map/ppermute | solution.py:31
  30.1 10.7 %collective-permute-start = (bf16[72,1024]{1,0:T(8,128)(2,1)S(1)}, bf16[72,1024]{1,0:T(8,128)(2,1)S(1)}, u32[]{:S(2)}, u32[]{:S(2)}) collective-permute-start(bf16[72,1024]{1,0:T(8,128)(2,1)S(1)} %slice.180.refs_0_), channel_id=1, source_target_pairs={{0,224},{32,0},{64,32},{96,64},{128,96},{160,128},{192,160},{224,1... | collective-permute-start | bytes 442376 | tf_op jit(solution)/shard_map/ppermute | solution.py:31
  30.9 38.8 %copy-start = (bf16[1024,2304]{1,0:T(8,128)(2,1)S(1)}, bf16[1024,2304]{1,0:T(8,128)(2,1)}, u32[]{:S(2)}) copy-start(bf16[1024,2304]{1,0:T(8,128)(2,1)} %refs_0_.2) | copy-start | bytes 14155780
  31.7 9.1 %collective-permute-start.6 = (bf16[72,1024]{1,0:T(8,128)(2,1)S(1)}, bf16[72,1024]{1,0:T(8,128)(2,1)S(1)}, u32[]{:S(2)}, u32[]{:S(2)}) collective-permute-start(bf16[72,1024]{1,0:T(8,128)(2,1)S(1)} %collective-permute-done.2.refs_3_), channel_id=1, source_target_pairs={{0,192},{32,224},{64,0},{96,32},{128,64},{160,96},{192,128},{224,1... | collective-permute-start | bytes 442376 | tf_op jit(solution)/shard_map/ppermute | solution.py:31
  33.5 0.7 copy-start.7
  38.9 1.9 %copy-start.8 = (bf16[4,448,1024]{2,1,0:T(8,128)(2,1)}, bf16[4,448,1024]{2,1,0:T(8,128)(2,1)S(1)}, u32[]{:S(2)}) copy-start(bf16[4,448,1024]{2,1,0:T(8,128)(2,1)S(1)} %get-tuple-element.33) | copy-start | bytes 11010052
  40.8 8.9 %collective-permute-start.13 = (f32[4,8,448]{2,1,0:T(8,128)S(1)}, f32[4,8,448]{2,1,0:T(8,128)S(1)}, u32[]{:S(2)}, u32[]{:S(2)}) collective-permute-start(f32[4,8,448]{2,1,0:T(8,128)S(1)} %get-tuple-element.34), channel_id=1, source_target_pairs={{0,16},{8,24},{16,0},{24,8},{1,17},{9,25},{17,1},{25,9},{2,18},{10... | collective-permute-start | bytes 172040 | tf_op jit(solution)/shard_map/ppermute | solution.py:31
  43.7 6.1 %collective-permute-start.12 = (f32[4,8,448]{2,1,0:T(8,128)S(1)}, f32[4,8,448]{2,1,0:T(8,128)S(1)}, u32[]{:S(2)}, u32[]{:S(2)}) collective-permute-start(f32[4,8,448]{2,1,0:T(8,128)S(1)} %get-tuple-element.34), channel_id=1, source_target_pairs={{0,8},{8,16},{16,24},{24,0},{1,9},{9,17},{17,25},{25,1},{2,10},{10... | collective-permute-start | bytes 172040 | tf_op jit(solution)/shard_map/ppermute | solution.py:31
  44.0 5.8 %collective-permute-start.11 = (f32[4,8,448]{2,1,0:T(8,128)S(1)}, f32[4,8,448]{2,1,0:T(8,128)S(1)}, u32[]{:S(2)}, u32[]{:S(2)}) collective-permute-start(f32[4,8,448]{2,1,0:T(8,128)S(1)} %get-tuple-element.34), channel_id=1, source_target_pairs={{0,24},{8,0},{16,8},{24,16},{1,25},{9,1},{17,9},{25,17},{2,26},{10... | collective-permute-start | bytes 172040 | tf_op jit(solution)/shard_map/ppermute | solution.py:31
  47.0 28.7 %collective-permute-start.8 = (bf16[576,1024]{1,0:T(8,128)(2,1)S(1)}, bf16[576,1024]{1,0:T(8,128)(2,1)S(1)}, u32[]{:S(2)}, u32[]{:S(2)}) collective-permute-start(bf16[576,1024]{1,0:T(8,128)(2,1)S(1)} %bitcast.43), channel_id=1, source_target_pairs={{0,8},{8,16},{16,24},{24,0},{1,9},{9,17},{17,25},{25,1},{2,10},{10... | collective-permute-start | bytes 3538952 | tf_op jit(solution)/shard_map/ppermute | solution.py:31
  47.1 29.5 %collective-permute-start.7 = (bf16[576,1024]{1,0:T(8,128)(2,1)S(1)}, bf16[576,1024]{1,0:T(8,128)(2,1)S(1)}, u32[]{:S(2)}, u32[]{:S(2)}) collective-permute-start(bf16[576,1024]{1,0:T(8,128)(2,1)S(1)} %bitcast.44), channel_id=1, source_target_pairs={{0,24},{8,0},{16,8},{24,16},{1,25},{9,1},{17,9},{25,17},{2,26},{10... | collective-permute-start | bytes 3538952 | tf_op jit(solution)/shard_map/ppermute | solution.py:31
  50.0 8.7 %collective-permute-start.20 = (f32[4,8,448]{2,1,0:T(8,128)S(1)}, f32[4,8,448]{2,1,0:T(8,128)S(1)}, u32[]{:S(2)}, u32[]{:S(2)}) collective-permute-start(f32[4,8,448]{2,1,0:T(8,128)S(1)} %select_select_fusion.1), channel_id=1, source_target_pairs={{0,128},{32,160},{64,192},{96,224},{128,0},{160,32},{192,64},{224,... | collective-permute-start | bytes 172040 | tf_op jit(solution)/shard_map/ppermute | solution.py:31
  54.2 10.1 %collective-permute-start.19 = (f32[4,8,448]{2,1,0:T(8,128)S(1)}, f32[4,8,448]{2,1,0:T(8,128)S(1)}, u32[]{:S(2)}, u32[]{:S(2)}) collective-permute-start(f32[4,8,448]{2,1,0:T(8,128)S(1)} %select_select_fusion.1), channel_id=1, source_target_pairs={{0,96},{32,128},{64,160},{96,192},{128,224},{160,0},{192,32},{224,... | collective-permute-start | bytes 172040 | tf_op jit(solution)/shard_map/ppermute | solution.py:31
  54.3 10.1 %collective-permute-start.18 = (f32[4,8,448]{2,1,0:T(8,128)S(1)}, f32[4,8,448]{2,1,0:T(8,128)S(1)}, u32[]{:S(2)}, u32[]{:S(2)}) collective-permute-start(f32[4,8,448]{2,1,0:T(8,128)S(1)} %select_select_fusion.1), channel_id=1, source_target_pairs={{0,160},{32,192},{64,224},{96,0},{128,32},{160,64},{192,96},{224,1... | collective-permute-start | bytes 172040 | tf_op jit(solution)/shard_map/ppermute | solution.py:31
  58.7 10.9 %collective-permute-start.17 = (f32[4,8,448]{2,1,0:T(8,128)S(1)}, f32[4,8,448]{2,1,0:T(8,128)S(1)}, u32[]{:S(2)}, u32[]{:S(2)}) collective-permute-start(f32[4,8,448]{2,1,0:T(8,128)S(1)} %select_select_fusion.1), channel_id=1, source_target_pairs={{0,64},{32,96},{64,128},{96,160},{128,192},{160,224},{192,0},{224,... | collective-permute-start | bytes 172040 | tf_op jit(solution)/shard_map/ppermute | solution.py:31
  64.2 11.0 %collective-permute-start.16 = (f32[4,8,448]{2,1,0:T(8,128)S(1)}, f32[4,8,448]{2,1,0:T(8,128)S(1)}, u32[]{:S(2)}, u32[]{:S(2)}) collective-permute-start(f32[4,8,448]{2,1,0:T(8,128)S(1)} %select_select_fusion.1), channel_id=1, source_target_pairs={{0,192},{32,224},{64,0},{96,32},{128,64},{160,96},{192,128},{224,1... | collective-permute-start | bytes 172040 | tf_op jit(solution)/shard_map/ppermute | solution.py:31
  64.5 10.8 %collective-permute-start.15 = (f32[4,8,448]{2,1,0:T(8,128)S(1)}, f32[4,8,448]{2,1,0:T(8,128)S(1)}, u32[]{:S(2)}, u32[]{:S(2)}) collective-permute-start(f32[4,8,448]{2,1,0:T(8,128)S(1)} %select_select_fusion.1), channel_id=1, source_target_pairs={{0,32},{32,64},{64,96},{96,128},{128,160},{160,192},{192,224},{224... | collective-permute-start | bytes 172040 | tf_op jit(solution)/shard_map/ppermute | solution.py:31
  69.5 5.8 %collective-permute-start.14 = (f32[4,8,448]{2,1,0:T(8,128)S(1)}, f32[4,8,448]{2,1,0:T(8,128)S(1)}, u32[]{:S(2)}, u32[]{:S(2)}) collective-permute-start(f32[4,8,448]{2,1,0:T(8,128)S(1)} %select_select_fusion.1), channel_id=1, source_target_pairs={{0,224},{32,0},{64,32},{96,64},{128,96},{160,128},{192,160},{224,1... | collective-permute-start | bytes 172040 | tf_op jit(solution)/shard_map/ppermute | solution.py:31
  73.1 2.1 %copy-start.2 = (bf16[1024,2304]{1,0:T(8,128)(2,1)}, bf16[1024,2304]{1,0:T(8,128)(2,1)S(1)}, u32[]{:S(2)}) copy-start(bf16[1024,2304]{1,0:T(8,128)(2,1)S(1)} %columns_by_x.1.refs_0_) | copy-start | bytes 14155780
  75.6 1.3 copy-start.3
  76.6 23.8 %collective-permute-start.10 = (bf16[576,512]{1,0:T(8,128)(2,1)}, bf16[576,512]{1,0:T(8,128)(2,1)S(1)}, u32[]{:S(2)}, u32[]{:S(2)}) collective-permute-start(bf16[576,512]{1,0:T(8,128)(2,1)} %slice.182), channel_id=1, source_target_pairs={{0,8},{8,16},{16,24},{24,0},{1,9},{9,17},{17,25},{25,1},{2,10},{10... | collective-permute-start | bytes 1769480 | tf_op jit(solution)/shard_map/ppermute | solution.py:31
  76.9 1.2 copy-start.5
  76.9 23.5 %slice-start = ((s8[4718592]{0:T(1024)(128)(4,1)}), s8[524288]{0:T(1024)(128)(4,1)S(1)}, s32[]{:S(2)}) async-start(s8[4718592]{0:T(1024)(128)(4,1)} %bitcast.41), calls=%async_computation.2 | async-start | bytes 1048576
  78.1 22.3 %collective-permute-start.9 = (bf16[576,512]{1,0:T(8,128)(2,1)}, bf16[576,512]{1,0:T(8,128)(2,1)}, u32[]{:S(2)}, u32[]{:S(2)}) collective-permute-start(bf16[576,512]{1,0:T(8,128)(2,1)} %slice.181), channel_id=1, source_target_pairs={{0,24},{8,0},{16,8},{24,16},{1,25},{9,1},{17,9},{25,17},{2,26},{10... | collective-permute-start | bytes 1769480 | tf_op jit(solution)/shard_map/ppermute | solution.py:31
  90.3 2.3 %copy-start.1 = (bf16[1024,2304]{1,0:T(8,128)(2,1)S(1)}, bf16[1024,2304]{1,0:T(8,128)(2,1)}, u32[]{:S(2)}) copy-start(bf16[1024,2304]{1,0:T(8,128)(2,1)} %refs_0_.2) | copy-start | bytes 14155780
  92.6 7.8 %slice-start.1 = ((s8[4718592]{0:T(1024)(128)(4,1)}), s8[4194304]{0:T(1024)(128)(4,1)S(1)}, s32[]{:S(2)}) async-start(s8[4718592]{0:T(1024)(128)(4,1)} %bitcast.41), calls=%async_computation.3 | async-start | bytes 8388608
  92.6 7.8 %copy-start.4 = (bf16[576,1024]{1,0:T(8,128)(2,1)S(1)}, bf16[576,1024]{1,0:T(8,128)(2,1)}, u32[]{:S(2)}) copy-start(bf16[576,1024]{1,0:T(8,128)(2,1)} %copy-done.3) | copy-start | bytes 3538948
  92.6 7.8 %copy-start.6 = (bf16[576,1024]{1,0:T(8,128)(2,1)S(1)}, bf16[576,1024]{1,0:T(8,128)(2,1)}, u32[]{:S(2)}) copy-start(bf16[576,1024]{1,0:T(8,128)(2,1)} %copy-done.5) | copy-start | bytes 3538948
  110.6 23.5 %all-to-all-start = ((f32[256,1,128]{2,1,0:T(1,128)}), f32[256,1,128]{2,1,0:T(1,128)S(1)}, u32[]{:S(2)}, u32[]{:S(2)}) async-start(f32[256,1,128]{2,1,0:T(1,128)} %bitcast.12), calls=%async_computation | async-start | bytes 262144 | tf_op jit(solution)/shard_map/all_to_all | solution.py:285
Sparse Core Ops, SparseCore 0:
  28.3 61.9 all-gather.1
